TPU v7x, 32 devices: a whole 2x2x4 slice. The times are simulated.
32 devices in a mesh: energy: 2 (over x), mom: 16 (over z, y, core).
Axes of the slice: x: 2, y: 2, z: 4, core: 2. Of those that a mesh axis runs over, the one named last changes fastest.
Arguments:
- source: float32 [256, 128, 1024], P(('energy', 'mom')), parts along dimension 0, may hold values from -6 to 6
- green: float32 [256, 1024], P(('energy', 'mom')), parts along dimension 0, may hold values from 0.1 to 0.6
- couple_one: float32 [2, 4, 128, 128], replicated, may hold values from -0.5 to 0.5
- couple_two: float32 [2, 4, 128, 128], replicated, may hold values from -0.5 to 0.5
- p_bracket: int32 [2, 1024], replicated, may hold values from 0 to 28
- q_bracket: int32 [2, 1024], replicated, may hold values from 0 to 28
- p_weight: float32 [2, 4, 1024], replicated, may hold values from -0.25 to 1
- q_weight: float32 [2, 4, 1024], replicated, may hold values from -0.25 to 1
- qr_bracket: int32 [2, 1024], replicated, may hold values from 0 to 28
- r_bracket: int32 [2, 1024], replicated, may hold values from 0 to 28
- qr_weight: float32 [2, 4, 1024], replicated, may hold values from -0.25 to 1
- r_weight: float32 [2, 4, 1024], replicated, may hold values from -0.25 to 1
Outputs:
- amplitude: float32 [256, 128, 1024], P(('energy', 'mom')), parts along dimension 0
- component: float32 [256, 128, 1024], P(('energy', 'mom')), parts along dimension 0
There are 2 independent parts, one for each index of `energy`. A program takes and returns all parts, laid end to end along the dimension named above; an argument that names none is the same for every part. Nothing has to cross between parts.
All inputs are finite; a program needn't handle non-finite values.
Results may differ from a plain program's by a relative error of at most 0.0001.
Values sent between devices are 32-bit elements; how exact they have to be, the bound alone decides.
No kernel may reach another device: no remote copies, remote signals or barrier semaphores. Data moves between devices by JAX's collectives and lax.ppermute only.
A program may use at most 128 MiB of HBM per device.

v0:
```python
import jax
import jax.numpy as jnp
from jax import lax
from jax.sharding import PartitionSpec as P

P_SIZE = 32
Q = 32
R = 32
K = 2
ITERS = 2


def spline_matrix(
    first_index, second_index, first_weight, second_weight, first_count, second_count
):
    first_grid = jnp.arange(first_count, dtype=jnp.int32)[None, :] - first_index[:, None]
    second_grid = jnp.arange(second_count, dtype=jnp.int32)[None, :] - second_index[:, None]
    first_rows = jnp.zeros(first_grid.shape, jnp.float32)
    second_rows = jnp.zeros(second_grid.shape, jnp.float32)
    for offset in range(4):
        first_rows = first_rows + jnp.where(
            first_grid == offset, first_weight[offset][:, None], jnp.float32(0.0)
        )
        second_rows = second_rows + jnp.where(
            second_grid == offset, second_weight[offset][:, None], jnp.float32(0.0)
        )
    return (first_rows[:, :, None] * second_rows[:, None, :]).reshape(
        first_index.shape[0], first_count * second_count
    )


def class_mats(couple, row_count, start):
    classes = (start + jnp.arange(row_count, dtype=jnp.int32)) % 4
    select = jax.nn.one_hot(classes, 4, dtype=jnp.float32)
    return jnp.einsum("rc,cmn->rmn", select, couple, precision=lax.Precision.HIGHEST)


def mix(mats, values):
    return jnp.einsum("rmn,rnx->rmx", mats, values, precision=lax.Precision.HIGHEST)


def interp(values, smat):
    return jnp.einsum("rcx,yx->rcy", values, smat, precision=lax.Precision.HIGHEST)


def to_send_one(values, quarter):
    rows = values.shape[0]
    return (
        values.reshape(rows, 4, quarter, P_SIZE, Q)
        .transpose(3, 1, 0, 2, 4)
        .reshape(4 * P_SIZE, rows, quarter * Q)
    )


def from_send_one(arrived, quarter):
    rows = arrived.shape[0]
    return (
        arrived.reshape(rows, R, 4, quarter, Q)
        .transpose(0, 3, 2, 4, 1)
        .reshape(rows, 4 * quarter, Q * R)
    )


def to_send_two(values, quarter):
    rows = values.shape[0]
    return (
        values.reshape(rows, quarter, 4, Q, R)
        .transpose(4, 2, 0, 1, 3)
        .reshape(4 * R, rows, quarter * Q)
    )


def from_send_two(arrived, quarter):
    rows = arrived.shape[0]
    return (
        arrived.reshape(rows, P_SIZE, 4, quarter, Q)
        .transpose(0, 2, 3, 1, 4)
        .reshape(rows, 4 * quarter, P_SIZE * Q)
    )


def shards(
    source,
    green,
    couple_one,
    couple_two,
    p_bracket,
    q_bracket,
    p_weight,
    q_weight,
    qr_bracket,
    r_bracket,
    qr_weight,
    r_weight,
):
    rows_one = source.shape[0]
    rows_two = green.shape[0]
    quarter = source.shape[1] // 4
    here = lax.axis_index("mom")
    first_maps = [
        spline_matrix(p_bracket[k], q_bracket[k], p_weight[k], q_weight[k], P_SIZE, Q)
        for k in range(K)
    ]
    second_maps = [
        spline_matrix(qr_bracket[k], r_bracket[k], qr_weight[k], r_weight[k], Q, R)
        for k in range(K)
    ]
    mats_one = [class_mats(couple_one[k], rows_one, here * rows_one) for k in range(K)]
    mats_two = [class_mats(couple_two[k], rows_two, here * rows_two) for k in range(K)]
    scale = green[:, None, :]
    state = source
    component = None
    for step in range(ITERS):
        one = interp(mix(mats_one[0], state), first_maps[0])
        k = 1
        one = one + interp(mix(mats_one[k], state), first_maps[k])
        arrived = lax.all_to_all(
            to_send_one(one, quarter), "mom", split_axis=0, concat_axis=1, tiled=True
        )
        regrouped = from_send_one(arrived, quarter)
        total = mix(mats_two[0], interp(regrouped, second_maps[0]))
        k = 1
        total = total + mix(mats_two[k], interp(regrouped, second_maps[k]))
        component = scale * total
        returned = lax.all_to_all(
            to_send_two(component, quarter), "mom", split_axis=0, concat_axis=1, tiled=True
        )
        state = source + from_send_two(returned, quarter)
    return (state, component)


def solution(mesh):
    placed = (
        P(("energy", "mom"), None, None),
        P(("energy", "mom"), None),
        P(),
        P(),
        P(),
        P(),
        P(),
        P(),
        P(),
        P(),
        P(),
        P(),
    )
    return jax.shard_map(
        shards,
        mesh=mesh,
        in_specs=placed,
        out_specs=(P(("energy", "mom"), None, None), P(("energy", "mom"), None, None)),
        check_vma=False,
    )
```

profile of v0, /device:TPU:9, one launch (start us, length us, event | category | flops | bytes accessed | tf_op | source)
XLA Modules:
  0.0 922.8 jit_solution(14042595359069601299)
XLA Ops:
  6.3 5.8 fusion.8
  12.2 4.1 fusion.14
  17.6 14.4 %fusion.68 = f32[8,128,1024]{2,1,0:T(8,128)S(1)} fusion(f32[8,128,1024]{2,1,0:T(8,128)S(1)} %fusion.8, f32[1024,1024,1]{0,1,2:T(8,128)S(1)} %bitcast.165), kind=kOutput, calls=%fused_computation.102 | convolution fusion | flops 12884901888 | bytes 12582912 | tf_op jit(solution)/shard_map/rcx,yx->rcy/dot_general | solution.py:43
  31.9 14.8 %convolution_add_fusion.1 = f32[8,128,1024]{2,1,0:T(8,128)} fusion(f32[8,128,1024]{2,1,0:T(8,128)S(1)} %fusion.68, f32[8,128,1024]{2,1,0:T(8,128)S(1)} %fusion.14, f32[1024,1024,1]{0,1,2:T(8,128)S(1)} %bitcast.156), kind=kOutput, calls=%fused_computation.13 | convolution fusion | flops 12885950464 | bytes 16777216 | tf_op jit(solution)/shard_map/rcx,yx->rcy/dot_general | solution.py:43
  46.8 11.6 %reshape.954 = f32[8,4,32,32,32]{4,3,2,1,0:T(8,128)} reshape(f32[8,128,1024]{2,1,0:T(8,128)} %convolution_add_fusion.1) | data formatting | bytes 8388608 | tf_op jit(solution)/shard_map/reshape | solution.py:49
  58.4 14.3 %copy.127 = f32[8,4,32,32,32]{4,2,0,1,3:T(8,128)} copy(f32[8,4,32,32,32]{4,3,2,1,0:T(8,128)} %reshape.954) | data formatting | bytes 8388608 | tf_op jit(solution)/shard_map/reshape | solution.py:49
  72.7 13.7 %reshape.955 = f32[128,8,1024]{2,1,0:T(8,128)} reshape(f32[32,4,8,32,32]{4,3,2,1,0:T(8,128)} %bitcast.148) | data formatting | bytes 8388608 | tf_op jit(solution)/shard_map/reshape | solution.py:51
  86.4 6.7 all-to-all-start
  97.2 2.6 broadcast_multiply_fusion
  99.8 83.5 %all-to-all-done = f32[128,8,1024]{2,1,0:T(8,128)} async-done(((f32[128,8,1024]{2,1,0:T(8,128)}), f32[128,8,1024]{2,1,0:T(8,128)}, u32[]{:S(2)}, u32[]{:S(2)}) %all-to-all-start) | async-done | bytes 4194336 | tf_op jit(solution)/shard_map/all_to_all | solution.py:117
  183.3 4.8 copy.131
  188.1 11.6 %reshape.956 = f32[8,32,4,32,32]{4,3,2,1,0:T(8,128)} reshape(f32[8,16,8,1024]{3,2,1,0:T(8,128)} %bitcast.158) | data formatting | bytes 8388608 | tf_op jit(solution)/shard_map/reshape | solution.py:58
  199.7 18.9 %copy.53 = f32[8,32,4,32,32]{4,3,2,1,0:T(8,128)} copy(f32[8,32,4,32,32]{3,1,2,4,0:T(8,128)} %bitcast.149) | data formatting | bytes 8388608 | tf_op jit(solution)/shard_map/transpose | solution.py:59
  218.6 13.7 %reshape.957 = f32[8,128,1024]{2,1,0:T(8,128)} reshape(f32[8,32,4,32,32]{4,3,2,1,0:T(8,128)} %copy.53) | data formatting | bytes 8388608 | tf_op jit(solution)/shard_map/reshape | solution.py:60
  232.3 17.2 %fusion.70 = f32[8,128,1024]{2,1,0:T(8,128)S(1)} fusion(f32[8,128,1024]{2,1,0:T(8,128)} %reshape.957, f32[1024,1024,1]{0,1,2:T(8,128)} %bitcast.169), kind=kOutput, calls=%fused_computation.104 | convolution fusion | flops 12884901888 | bytes 12582912 | tf_op jit(solution)/shard_map/rcx,yx->rcy/dot_general | solution.py:43
  249.5 13.4 %fusion.69 = f32[8,128,1024]{2,1,0:T(8,128)S(1)} fusion(f32[8,128,1024]{2,1,0:T(8,128)S(1)} %copy-done.6, f32[1024,1024,1]{0,1,2:T(8,128)S(1)} %bitcast.167), kind=kOutput, calls=%fused_computation.103 | convolution fusion | flops 12884901888 | bytes 12582912 | tf_op jit(solution)/shard_map/rcx,yx->rcy/dot_general | solution.py:43
  263.0 4.2 fusion.4
  267.2 5.2 add_multiply_fusion.1
  272.5 11.6 %reshape.958 = f32[8,32,4,32,32]{4,3,2,1,0:T(8,128)} reshape(f32[8,128,1024]{2,1,0:T(8,128)} %add_multiply_fusion.1) | data formatting | bytes 8388608 | tf_op jit(solution)/shard_map/reshape | solution.py:67
  284.1 20.0 %copy.59 = f32[8,32,4,32,32]{3,1,0,2,4:T(8,128)} copy(f32[8,32,4,32,32]{4,3,2,1,0:T(8,128)} %reshape.958) | data formatting | bytes 8388608 | tf_op jit(solution)/shard_map/reshape | solution.py:67
  304.1 13.7 %reshape.959 = f32[128,8,1024]{2,1,0:T(8,128)} reshape(f32[32,4,8,32,32]{4,3,2,1,0:T(8,128)} %bitcast.150) | data formatting | bytes 8388608 | tf_op jit(solution)/shard_map/reshape | solution.py:69
  317.8 100.0 %all_to_all.60 = f32[128,8,1024]{2,1,0:T(8,128)S(1)} all-to-all(f32[128,8,1024]{2,1,0:T(8,128)} %reshape.959), channel_id=1, replica_groups=mesh['energy'=2,'mom'=16] {'mom'}, dimensions={0} | all-to-all | bytes 8388608 | tf_op jit(solution)/shard_map/all_to_all | solution.py:125
  420.0 11.6 %reshape.960 = f32[8,32,4,32,32]{4,3,2,1,0:T(8,128)} reshape(f32[8,16,8,1024]{3,2,1,0:T(8,128)} %bitcast.159) | data formatting | bytes 8388608 | tf_op jit(solution)/shard_map/reshape | solution.py:76
  431.7 18.4 %copy.61 = f32[8,4,32,32,32]{4,3,2,1,0:T(8,128)} copy(f32[8,4,32,32,32]{4,2,1,3,0:T(8,128)} %bitcast.151) | data formatting | bytes 8388608 | tf_op jit(solution)/shard_map/transpose | solution.py:77
  450.1 13.7 %reshape.961 = f32[8,128,1024]{2,1,0:T(8,128)} reshape(f32[8,4,32,32,32]{4,3,2,1,0:T(8,128)} %copy.61) | data formatting | bytes 8388608 | tf_op jit(solution)/shard_map/reshape | solution.py:78
  463.8 6.4 fusion
  470.2 3.9 fusion.2
  474.1 14.2 %fusion.71 = f32[8,128,1024]{2,1,0:T(8,128)S(1)} fusion(f32[8,128,1024]{2,1,0:T(8,128)S(1)} %fusion.2, f32[1024,1024,1]{0,1,2:T(8,128)S(1)} %bitcast.166), kind=kOutput, calls=%fused_computation.105 | convolution fusion | flops 12884901888 | bytes 12582912 | tf_op jit(solution)/shard_map/rcx,yx->rcy/dot_general | solution.py:43
  488.3 14.8 %convolution_add_fusion = f32[8,128,1024]{2,1,0:T(8,128)} fusion(f32[8,128,1024]{2,1,0:T(8,128)S(1)} %fusion.71, f32[8,128,1024]{2,1,0:T(8,128)S(1)} %fusion, f32[1024,1024,1]{0,1,2:T(8,128)S(1)} %bitcast.157), kind=kOutput, calls=%fused_computation.12 | convolution fusion | flops 12885950464 | bytes 16777216 | tf_op jit(solution)/shard_map/rcx,yx->rcy/dot_general | solution.py:43
  503.2 11.6 %reshape.962 = f32[8,4,32,32,32]{4,3,2,1,0:T(8,128)} reshape(f32[8,128,1024]{2,1,0:T(8,128)} %convolution_add_fusion) | data formatting | bytes 8388608 | tf_op jit(solution)/shard_map/reshape | solution.py:49
  514.8 14.3 %copy.126 = f32[8,4,32,32,32]{4,2,0,1,3:T(8,128)} copy(f32[8,4,32,32,32]{4,3,2,1,0:T(8,128)} %reshape.962) | data formatting | bytes 8388608 | tf_op jit(solution)/shard_map/reshape | solution.py:49
  529.1 13.7 %reshape.963 = f32[128,8,1024]{2,1,0:T(8,128)} reshape(f32[32,4,8,32,32]{4,3,2,1,0:T(8,128)} %bitcast.152) | data formatting | bytes 8388608 | tf_op jit(solution)/shard_map/reshape | solution.py:51
  542.7 97.4 %all_to_all.61 = f32[128,8,1024]{2,1,0:T(8,128)S(1)} all-to-all(f32[128,8,1024]{2,1,0:T(8,128)} %reshape.963), channel_id=1, replica_groups=mesh['energy'=2,'mom'=16] {'mom'}, dimensions={0} | all-to-all | bytes 8388608 | tf_op jit(solution)/shard_map/all_to_all | solution.py:117
  642.5 11.6 %reshape.964 = f32[8,32,4,32,32]{4,3,2,1,0:T(8,128)} reshape(f32[8,16,8,1024]{3,2,1,0:T(8,128)} %bitcast.160) | data formatting | bytes 8388608 | tf_op jit(solution)/shard_map/reshape | solution.py:58
  654.1 18.9 %copy.68 = f32[8,32,4,32,32]{4,3,2,1,0:T(8,128)} copy(f32[8,32,4,32,32]{3,1,2,4,0:T(8,128)} %bitcast.153) | data formatting | bytes 8388608 | tf_op jit(solution)/shard_map/transpose | solution.py:59
  673.0 13.7 %reshape.965 = f32[8,128,1024]{2,1,0:T(8,128)} reshape(f32[8,32,4,32,32]{4,3,2,1,0:T(8,128)} %copy.68) | data formatting | bytes 8388608 | tf_op jit(solution)/shard_map/reshape | solution.py:60
  686.7 17.2 %fusion.73 = f32[8,128,1024]{2,1,0:T(8,128)S(1)} fusion(f32[8,128,1024]{2,1,0:T(8,128)} %reshape.965, f32[1024,1024,1]{0,1,2:T(8,128)} %bitcast.170), kind=kOutput, calls=%fused_computation.107 | convolution fusion | flops 12884901888 | bytes 12582912 | tf_op jit(solution)/shard_map/rcx,yx->rcy/dot_general | solution.py:43
  703.9 13.4 %fusion.72 = f32[8,128,1024]{2,1,0:T(8,128)S(1)} fusion(f32[8,128,1024]{2,1,0:T(8,128)S(1)} %copy-done.5, f32[1024,1024,1]{0,1,2:T(8,128)S(1)} %bitcast.168), kind=kOutput, calls=%fused_computation.106 | convolution fusion | flops 12884901888 | bytes 12582912 | tf_op jit(solution)/shard_map/rcx,yx->rcy/dot_general | solution.py:43
  717.4 4.2 fusion.6
  721.6 5.2 add_multiply_fusion
  726.8 11.6 %reshape.966 = f32[8,32,4,32,32]{4,3,2,1,0:T(8,128)} reshape(f32[8,128,1024]{2,1,0:T(8,128)} %add_multiply_fusion) | data formatting | bytes 8388608 | tf_op jit(solution)/shard_map/reshape | solution.py:67
  738.5 20.0 %copy.73 = f32[8,32,4,32,32]{3,1,0,2,4:T(8,128)} copy(f32[8,32,4,32,32]{4,3,2,1,0:T(8,128)} %reshape.966) | data formatting | bytes 8388608 | tf_op jit(solution)/shard_map/reshape | solution.py:67
  758.5 13.7 %reshape.967 = f32[128,8,1024]{2,1,0:T(8,128)} reshape(f32[32,4,8,32,32]{4,3,2,1,0:T(8,128)} %bitcast.154) | data formatting | bytes 8388608 | tf_op jit(solution)/shard_map/reshape | solution.py:69
  772.1 97.6 %all_to_all.62 = f32[128,8,1024]{2,1,0:T(8,128)S(1)} all-to-all(f32[128,8,1024]{2,1,0:T(8,128)} %reshape.967), channel_id=1, replica_groups=mesh['energy'=2,'mom'=16] {'mom'}, dimensions={0} | all-to-all | bytes 8388608 | tf_op jit(solution)/shard_map/all_to_all | solution.py:125
  872.0 11.6 %reshape.968 = f32[8,32,4,32,32]{4,3,2,1,0:T(8,128)} reshape(f32[8,16,8,1024]{3,2,1,0:T(8,128)} %bitcast.161) | data formatting | bytes 8388608 | tf_op jit(solution)/shard_map/reshape | solution.py:76
  883.7 18.4 %copy.75 = f32[8,4,32,32,32]{4,3,2,1,0:T(8,128)} copy(f32[8,4,32,32,32]{4,2,1,3,0:T(8,128)} %bitcast.155) | data formatting | bytes 8388608 | tf_op jit(solution)/shard_map/transpose | solution.py:77
  902.1 13.7 %reshape.969 = f32[8,128,1024]{2,1,0:T(8,128)} reshape(f32[8,4,32,32,32]{4,3,2,1,0:T(8,128)} %copy.75) | data formatting | bytes 8388608 | tf_op jit(solution)/shard_map/reshape | solution.py:78
  915.8 6.8 add.250
  (59 shorter events, 17.9 us)
Async XLA Ops:
  6.3 5.8 copy-start
  16.9 15.0 %copy-start.7 = (f32[1024,32,32]{0,2,1:T(8,128)}, f32[1024,32,32]{0,2,1:T(8,128)S(1)}, u32[]{:S(2)}) copy-start(f32[1024,32,32]{0,2,1:T(8,128)S(1)} %broadcast_multiply_fusion.3) | copy-start | bytes 12582916
  17.5 14.4 %copy-start.3 = (f32[1024,32,32]{0,2,1:T(8,128)}, f32[1024,32,32]{0,2,1:T(8,128)S(1)}, u32[]{:S(2)}) copy-start(f32[1024,32,32]{0,2,1:T(8,128)S(1)} %broadcast_multiply_fusion.2) | copy-start | bytes 12582916
  86.3 6.7 copy-start.15
  86.3 6.8 copy-start.16
  86.3 6.8 copy-start.13
  86.3 6.8 copy-start.14
  86.4 7.1 copy-start.11
  86.4 96.9 %all-to-all-start = ((f32[128,8,1024]{2,1,0:T(8,128)}), f32[128,8,1024]{2,1,0:T(8,128)}, u32[]{:S(2)}, u32[]{:S(2)}) async-start(f32[128,8,1024]{2,1,0:T(8,128)} %reshape.955), calls=%async_computation | async-start | bytes 8388608 | tf_op jit(solution)/shard_map/all_to_all | solution.py:117
  232.3 17.2 %copy-start.6 = (f32[8,128,1024]{2,1,0:T(8,128)S(1)}, f32[8,128,1024]{2,1,0:T(8,128)}, u32[]{:S(2)}) copy-start(f32[8,128,1024]{2,1,0:T(8,128)} %reshape.957) | copy-start | bytes 12582916
  232.3 17.3 %copy-start.9 = (f32[1024,32,32]{0,2,1:T(8,128)S(1)}, f32[1024,32,32]{0,2,1:T(8,128)}, u32[]{:S(2)}) copy-start(f32[1024,32,32]{0,2,1:T(8,128)} %broadcast_multiply_fusion.1) | copy-start | bytes 12582916
  263.0 4.3 copy-start.12
  463.8 6.4 copy-start.1
  463.8 6.4 copy-start.2
  470.2 4.0 copy-start.8
  474.1 14.2 %copy-start.4 = (f32[1024,32,32]{0,2,1:T(8,128)S(1)}, f32[1024,32,32]{0,2,1:T(8,128)}, u32[]{:S(2)}) copy-start(f32[1024,32,32]{0,2,1:T(8,128)} %copy-done.3) | copy-start | bytes 12582916
  686.7 17.2 %copy-start.5 = (f32[8,128,1024]{2,1,0:T(8,128)S(1)}, f32[8,128,1024]{2,1,0:T(8,128)}, u32[]{:S(2)}) copy-start(f32[8,128,1024]{2,1,0:T(8,128)} %reshape.965) | copy-start | bytes 12582916
  686.7 17.3 %copy-start.10 = (f32[1024,32,32]{0,2,1:T(8,128)S(1)}, f32[1024,32,32]{0,2,1:T(8,128)}, u32[]{:S(2)}) copy-start(f32[1024,32,32]{0,2,1:T(8,128)} %broadcast_multiply_fusion.1) | copy-start | bytes 12582916
where the time goes:
time: 932 us; the launch traced here: 923 us
  local copies, waits for them, and re-layouts  362 us (39%)
  blocking collectives  295 us (32%)
  matrix products  161 us (17%)
  waiting for transfers between devices  83.5 us (9%)
  other arithmetic  13.5 us (1%)
    all_to_all x2, blocking collectives, shards(): lax.all_to_all(to_send_two(component, quarter), 'mom', split_axis=0, conc...  198 us
    dot_general x8, matrix products, interp(): jnp.einsum('rcx,yx->rcy', values, smat, precision=lax.Precision.HIGHEST)  120 us
    all_to_all x1, blocking collectives, shards(): lax.all_to_all(to_send_one(one, quarter), 'mom', split_axis=0, concat_axi...  97.4 us
    all_to_all x1, waiting for transfers between devices, shards(): lax.all_to_all(to_send_one(one, quarter), 'mom', split_axis=0, concat_axi...  83.5 us
    reshape x4, local copies, waits for them, and re-layouts, to_send_two(): values.reshape(rows, quarter, 4, Q, R).transpose(4, 2, 0, 1, 3)  63.2 us
    reshape x4, local copies, waits for them, and re-layouts, to_send_one(): values.reshape(rows, 4, quarter, P_SIZE, Q).transpose(3, 1, 0, 2, 4)  51.8 us
    dot_general x8, matrix products, mix(): jnp.einsum('rmn,rnx->rmx', mats, values, precision=lax.Precision.HIGHEST)  39.1 us
    transpose x2, local copies, waits for them, and re-layouts, from_send_one(): return arrived.reshape(rows, R, 4, quarter, Q).transpose(0, 3, 2, 4, 1).r...  37.8 us
  transfers between devices with their start and end apart: 1, of which 1 were waited for; matrix products, arithmetic and copies ran while one was open for 1% of the time, Pallas kernels for 0%

commit v1 on v0

v1 whole, which is shorter than its diff:
```python
import functools

import jax
import jax.numpy as jnp
from jax import lax
from jax.experimental import pallas as pl
from jax.experimental.pallas import tpu as pltpu
from jax.sharding import PartitionSpec as P

ITERS = 2
LANES = 128
F32 = jnp.float32
BF16 = jnp.bfloat16


def split(value):
    high = value.astype(BF16)
    return high, (value - high.astype(F32)).astype(BF16)


def dot(a, b):
    return jnp.dot(a, b, preferred_element_type=F32)


def dot_nt(a, b):
    return lax.dot_general(a, b, (((1,), (1,)), ((), ())), preferred_element_type=F32)


def map_kernel(count, table_ref, high_ref, low_ref):
    table = table_ref[0]
    rows = table.shape[0]
    columns = high_ref.shape[1]
    lane = lax.broadcasted_iota(jnp.int32, (rows, LANES), 1)

    def factor(index, base):
        grid = index.astype(F32) - table[:, base : base + 1]
        total = jnp.zeros((rows, LANES), F32)
        for offset in range(4):
            column = 2 + 4 * base + offset
            total = total + jnp.where(grid == offset, table[:, column : column + 1], 0.0)
        return total

    shared = None
    for tile in range(columns // LANES):
        index = lane + tile * LANES
        if shared is None or LANES % count:
            shared = factor(lax.rem(index, count), 1)
        value = factor(lax.div(index, count), 0) * shared
        high, low = split(value)
        high_ref[:, tile * LANES : (tile + 1) * LANES] = high
        low_ref[:, tile * LANES : (tile + 1) * LANES] = low


def spline_maps(first, second, first_weight, second_weight, count):
    angles, size = first.shape
    table = jnp.concatenate(
        [
            first[..., None].astype(F32),
            second[..., None].astype(F32),
            first_weight.transpose(0, 2, 1),
            second_weight.transpose(0, 2, 1),
        ],
        axis=-1,
    )
    tile = min(256, size)
    out = jax.ShapeDtypeStruct((size, angles * size), BF16)
    spec = pl.BlockSpec((tile, size), lambda k, i: (i, k))
    return pl.pallas_call(
        functools.partial(map_kernel, count),
        grid=(angles, size // tile),
        in_specs=[pl.BlockSpec((1, tile, table.shape[2]), lambda k, i: (k, i, 0))],
        out_specs=[spec, spec],
        out_shape=[out, out],
        cost_estimate=pl.CostEstimate(
            flops=20 * angles * size * size,
            bytes_accessed=4 * angles * size * size,
            transcendentals=0,
        ),
        name="spline_maps",
    )(table)


def turn_kernel(quarter, source_ref, out_ref):
    for g in range(4):
        rows = [source_ref[c, g * quarter : (g + 1) * quarter, :] for c in range(4)]
        out_ref[g, 0] = jnp.concatenate(rows, axis=0).T


def turn_source(source):
    rows, channels, size = source.shape
    tile = min(256, size)
    return pl.pallas_call(
        functools.partial(turn_kernel, channels // 4),
        grid=(rows // 4, size // tile),
        in_specs=[pl.BlockSpec((4, channels, tile), lambda r, i: (r, 0, i))],
        out_specs=pl.BlockSpec((4, 1, tile, channels), lambda r, i: (0, r, i, 0)),
        out_shape=jax.ShapeDtypeStruct((4, rows // 4, size, channels), F32),
        cost_estimate=pl.CostEstimate(
            flops=0, bytes_accessed=8 * source.size, transcendentals=0
        ),
        name="turn_source",
    )(source)


def interpolate(high_ref, low_ref, mixed_high, mixed_low):
    high = high_ref[...]
    return (
        dot(high, mixed_high[...]) + dot(high, mixed_low[...]) + dot(low_ref[...], mixed_high[...])
    )


def one_kernel(g, arrived, base_ref, *refs):
    backs = refs[:arrived]
    couple_ref, high_ref, low_ref, out_ref, w_high, w_low, m_high, m_low = refs[arrived:]
    angles, _, channels, _ = couple_ref.shape
    quarter = channels // 4
    _, local, size, _ = base_ref.shape

    @pl.when(pl.program_id(0) == 0)
    def _():
        lane = lax.broadcasted_iota(jnp.int32, (quarter, channels), 1)
        for k in range(angles):
            for c in range(4):
                rows = couple_ref[k, c, g * quarter : (g + 1) * quarter, :]
                at = k * channels + c * quarter
                inside = lax.div(lane, quarter) == c
                for other in range(4):
                    shift = ((c - other) * quarter) % channels
                    moved = pltpu.roll(rows, shift, 1) if shift else rows
                    high, low = split(jnp.where(inside, moved, 0.0))
                    w_high[at : at + quarter, other * channels : (other + 1) * channels] = high
                    w_low[at : at + quarter, other * channels : (other + 1) * channels] = low
        tile = min(256, size)
        per = backs[0].shape[2] if arrived else 0

        for r in range(local):

            def step(i, carry, r=r):
                start = pl.multiple_of(i * tile, tile)
                parts = []
                for other in range(4):
                    part = base_ref[other, r, pl.ds(start, tile), :]
                    if arrived:
                        block = backs[other][pl.ds(i * (tile // per), tile // per), r]
                        part = part + block.reshape(tile, channels)
                    parts.append(part)
                high, low = split(jnp.concatenate(parts, axis=1))
                mixed = (
                    dot_nt(high, w_high[...]) + dot_nt(high, w_low[...]) + dot_nt(low, w_high[...])
                )
                high, low = split(mixed)
                for k in range(angles):
                    lanes = slice(k * channels, (k + 1) * channels)
                    rows = pl.ds(pl.multiple_of(k * size + i * tile, tile), tile)
                    m_high[rows, r * channels : (r + 1) * channels] = high[:, lanes]
                    m_low[rows, r * channels : (r + 1) * channels] = low[:, lanes]
                return carry

            lax.fori_loop(0, size // tile, step, 0)

    value = interpolate(high_ref, low_ref, m_high, m_low)
    parts, near, _, count, _ = out_ref.shape
    for r in range(local):
        block = value[:, r * channels : (r + 1) * channels]
        out_ref[:, :, r, :, :] = block.reshape(parts, near, count, channels)


def component_one(g, base, backs, couple, maps, near, devices):
    _, local, size, channels = base.shape
    angles = couple.shape[0]
    steps = 4
    count = size // (devices * near)
    arrived = len(backs)
    out = (devices, near, local, count, channels)
    products = 3 * 2 * local * channels * angles * size
    return pl.pallas_call(
        functools.partial(one_kernel, g, arrived),
        grid=(steps,),
        in_specs=[pl.BlockSpec(base.shape, lambda i: (0, 0, 0, 0))]
        + [pl.BlockSpec(back.shape, lambda i: (0, 0, 0, 0)) for back in backs]
        + [pl.BlockSpec(couple.shape, lambda i: (0, 0, 0, 0))]
        + [pl.BlockSpec((size // steps, angles * size), lambda i: (i, 0))] * 2,
        out_specs=pl.BlockSpec((devices // steps,) + out[1:], lambda i: (i, 0, 0, 0, 0)),
        out_shape=jax.ShapeDtypeStruct(out, F32),
        scratch_shapes=[pltpu.VMEM((angles * channels, 4 * channels), BF16)] * 2
        + [pltpu.VMEM((angles * size, local * channels), BF16)] * 2,
        compiler_params=pltpu.CompilerParams(vmem_limit_bytes=48 << 20),
        cost_estimate=pl.CostEstimate(
            flops=products * (size + 4 * channels),
            bytes_accessed=4 * base.size + 4 * angles * size * size,
            transcendentals=0,
        ),
        name="component_one",
    )(base, *backs, couple, *maps)


def two_kernel(x_ref, couple_ref, green_ref, high_ref, low_ref, out_ref, m_high, m_low):
    angles, channels, _ = couple_ref.shape
    devices, local, per, _ = x_ref.shape
    size = devices * per

    @pl.when(pl.program_id(0) == 0)
    def _():
        w_high, w_low = split(couple_ref[...].reshape(angles * channels, channels))
        tile = min(256, size)
        for p in range(local):

            def step(i, carry, p=p):
                block = x_ref[pl.ds(i * (tile // per), tile // per), p]
                high, low = split(block.reshape(tile, channels))
                mixed = dot_nt(high, w_high) + dot_nt(high, w_low) + dot_nt(low, w_high)
                high, low = split(mixed)
                for k in range(angles):
                    lanes = slice(k * channels, (k + 1) * channels)
                    rows = pl.ds(pl.multiple_of(k * size + i * tile, tile), tile)
                    m_high[rows, p * channels : (p + 1) * channels] = high[:, lanes]
                    m_low[rows, p * channels : (p + 1) * channels] = low[:, lanes]
                return carry

            lax.fori_loop(0, size // tile, step, 0)

    value = interpolate(high_ref, low_ref, m_high, m_low)
    parts, near, _, count, _ = out_ref.shape
    for p in range(local):
        block = value[:, p * channels : (p + 1) * channels] * green_ref[:, p : p + 1]
        out_ref[:, :, p, :, :] = block.reshape(parts, near, count, channels)


def component_two(g, arrived, couple, green, maps, near):
    devices, local, per, channels = arrived.shape
    size = devices * per
    angles = couple.shape[0]
    steps = 4
    out = (devices, near, local, per // near, channels)
    products = 3 * 2 * local * channels * angles * size
    return pl.pallas_call(
        two_kernel,
        grid=(steps,),
        in_specs=[
            pl.BlockSpec(arrived.shape, lambda i: (0, 0, 0, 0)),
            pl.BlockSpec((angles, None, channels, channels), lambda i: (0, g, 0, 0)),
            pl.BlockSpec((None, size // steps, local), lambda i: (g, i, 0)),
        ]
        + [pl.BlockSpec((size // steps, angles * size), lambda i: (i, 0))] * 2,
        out_specs=pl.BlockSpec((devices // steps,) + out[1:], lambda i: (i, 0, 0, 0, 0)),
        out_shape=jax.ShapeDtypeStruct(out, F32),
        scratch_shapes=[pltpu.VMEM((angles * size, local * channels), BF16)] * 2,
        compiler_params=pltpu.CompilerParams(vmem_limit_bytes=48 << 20),
        cost_estimate=pl.CostEstimate(
            flops=products * (size + channels),
            bytes_accessed=4 * arrived.size + 4 * angles * size * size,
            transcendentals=0,
        ),
        name="component_two",
    )(arrived, couple, green, *maps)


def amplitude_kernel(quarter, source_ref, back_ref, *refs):
    out_ref = refs[-1]
    back = back_ref[...]
    turned = back.reshape(-1, back.shape[-1]).T
    for c in range(4):
        out_ref[c] = source_ref[c] + turned[c * quarter : (c + 1) * quarter]


def amplitude_chunk(g, source, back, so_far):
    rows, channels, size = source.shape
    devices, local, per, _ = back.shape
    quarter = channels // 4
    tile = min(512, size)
    spec = pl.BlockSpec((4, quarter, tile), lambda r, i: (r, g, i))
    in_specs = [
        spec,
        pl.BlockSpec((tile // per, None, per, channels), lambda r, i: (i, r, 0, 0)),
    ]
    args = [source, back]
    aliases = {}
    if so_far is not None:
        in_specs.append(pl.BlockSpec(memory_space=pl.ANY))
        args.append(so_far)
        aliases = {2: 0}
    return pl.pallas_call(
        functools.partial(amplitude_kernel, quarter),
        grid=(local, size // tile),
        in_specs=in_specs,
        out_specs=spec,
        out_shape=jax.ShapeDtypeStruct(source.shape, F32),
        input_output_aliases=aliases,
        cost_estimate=pl.CostEstimate(
            flops=back.size, bytes_accessed=12 * back.size, transcendentals=0
        ),
        name="amplitude",
    )(*args)


def output_kernel(quarter, sent_ref, *refs):
    out_ref, turned_ref = refs[-2:]
    devices, near, count, channels = sent_ref.shape
    per_tile = LANES // (devices * near)
    for tile in range(count // per_tile):
        rows = [
            sent_ref[:, :, tile * per_tile + i, :].reshape(devices * near, channels)
            for i in range(per_tile)
        ]
        turned = jnp.concatenate(rows, axis=0).T
        for c in range(4):
            turned_ref[tile, pl.ds(c, quarter, stride=4), :] = turned[
                c * quarter : (c + 1) * quarter
            ]
        out_ref[:, tile * LANES : (tile + 1) * LANES] = turned_ref[tile]


def component_chunk(g, sent, so_far):
    devices, near, local, count, channels = sent.shape
    size = devices * near * count
    in_specs = [
        pl.BlockSpec((devices, near, None, count, channels), lambda p: (0, 0, p, 0, 0))
    ]
    args = [sent]
    aliases = {}
    if so_far is not None:
        in_specs.append(pl.BlockSpec(memory_space=pl.ANY))
        args.append(so_far)
        aliases = {1: 0}
    return pl.pallas_call(
        functools.partial(output_kernel, channels // 4),
        grid=(local,),
        in_specs=in_specs,
        out_specs=pl.BlockSpec((None, channels, size), lambda p: (4 * p + g, 0, 0)),
        out_shape=jax.ShapeDtypeStruct((4 * local, channels, size), F32),
        scratch_shapes=[pltpu.VMEM((size // LANES, channels, LANES), F32)],
        input_output_aliases=aliases,
        cost_estimate=pl.CostEstimate(
            flops=0, bytes_accessed=8 * sent.size, transcendentals=0
        ),
        name="component_out",
    )(*args)


def exchange(values):
    devices, near, local, count, channels = values.shape
    sent = values.reshape(devices, near, local * count, channels)
    return lax.all_to_all(sent, "mom", split_axis=0, concat_axis=0, tiled=True)


def shards(
    devices,
    source,
    green,
    couple_one,
    couple_two,
    p_bracket,
    q_bracket,
    p_weight,
    q_weight,
    qr_bracket,
    r_bracket,
    qr_weight,
    r_weight,
):
    rows_one, channels, size_one = source.shape
    rows_two, size_two = green.shape
    angles = couple_one.shape[0]
    quarter = channels // 4
    near_r, near_p = rows_one // 4, rows_two // 4
    r_size, p_size = devices * near_r, devices * near_p
    q_size = size_one // p_size

    base = turn_source(source)
    first_maps = spline_maps(p_bracket, q_bracket, p_weight, q_weight, q_size)

    def by_r(array):
        lead = array.shape[:-1]
        return array.reshape(lead + (q_size, r_size)).swapaxes(-1, -2).reshape(lead + (-1,))

    second_maps = spline_maps(
        by_r(r_bracket), by_r(qr_bracket), by_r(r_weight), by_r(qr_weight), q_size
    )
    couple_two = (
        couple_two.reshape(angles, 4, quarter, 4, quarter, 4)
        .transpose(0, 1, 3, 2, 5, 4)
        .reshape(couple_two.shape)
    )
    green = (
        green.reshape(near_p, 4, q_size, r_size)
        .transpose(1, 3, 2, 0)
        .reshape(4, size_two, near_p)
    )
    backs = []
    for step in range(ITERS):
        ones = [
            exchange(component_one(g, base, backs, couple_one, first_maps, near_p, devices))
            for g in range(4)
        ]
        twos = [
            component_two(g, ones[g], couple_two, green, second_maps, near_r) for g in range(4)
        ]
        backs = [exchange(two) for two in twos]
    component = None
    for g in range(4):
        component = component_chunk(g, twos[g], component)
    amplitude = None
    for g in range(4):
        amplitude = amplitude_chunk(g, source, backs[g], amplitude)
    return amplitude, component


def whole_map(first, second, first_weight, second_weight, first_count, second_count):
    first_rows = jnp.zeros((first.shape[0], first_count), F32)
    second_rows = jnp.zeros((second.shape[0], second_count), F32)
    first_grid = jnp.arange(first_count, dtype=jnp.int32)[None, :] - first[:, None]
    second_grid = jnp.arange(second_count, dtype=jnp.int32)[None, :] - second[:, None]
    for offset in range(4):
        first_rows += jnp.where(first_grid == offset, first_weight[offset][:, None], 0.0)
        second_rows += jnp.where(second_grid == offset, second_weight[offset][:, None], 0.0)
    return (first_rows[:, :, None] * second_rows[:, None, :]).reshape(first.shape[0], -1)


def row_mats(couple, rows, start):
    select = jax.nn.one_hot((start + jnp.arange(rows, dtype=jnp.int32)) % 4, 4, dtype=F32)
    return jnp.einsum("rc,kcmn->krmn", select, couple, precision=lax.Precision.HIGHEST)


def mix_rows(mats, values):
    return jnp.einsum("rmn,rnx->rmx", mats, values, precision=lax.Precision.HIGHEST)


def interpolate_rows(values, matrix):
    return jnp.einsum("rcx,yx->rcy", values, matrix, precision=lax.Precision.HIGHEST)


def shards_by_row(
    devices,
    source,
    green,
    couple_one,
    couple_two,
    p_bracket,
    q_bracket,
    p_weight,
    q_weight,
    qr_bracket,
    r_bracket,
    qr_weight,
    r_weight,
):
    rows_one, channels, size_one = source.shape
    rows_two, size_two = green.shape
    angles = couple_one.shape[0]
    quarter = channels // 4
    r_size, p_size = devices * rows_one // 4, devices * rows_two // 4
    q_size = size_one // p_size
    here = lax.axis_index("mom")
    first = [
        whole_map(p_bracket[k], q_bracket[k], p_weight[k], q_weight[k], p_size, q_size)
        for k in range(angles)
    ]
    second = [
        whole_map(qr_bracket[k], r_bracket[k], qr_weight[k], r_weight[k], q_size, r_size)
        for k in range(angles)
    ]
    mats_one = row_mats(couple_one, rows_one, here * rows_one)
    mats_two = row_mats(couple_two, rows_two, here * rows_two)
    state = source
    for step in range(ITERS):
        one = sum(interpolate_rows(mix_rows(mats_one[k], state), first[k]) for k in range(angles))
        sent = one.reshape(rows_one, 4, quarter, p_size, q_size).transpose(3, 1, 0, 2, 4)
        sent = sent.reshape(4 * p_size, rows_one, quarter * q_size)
        sent = lax.all_to_all(sent, "mom", split_axis=0, concat_axis=1, tiled=True)
        sent = sent.reshape(rows_two, r_size, 4, quarter, q_size).transpose(0, 3, 2, 4, 1)
        sent = sent.reshape(rows_two, channels, size_two)
        total = sum(mix_rows(mats_two[k], interpolate_rows(sent, second[k])) for k in range(angles))
        component = green[:, None, :] * total
        back = component.reshape(rows_two, quarter, 4, q_size, r_size).transpose(4, 2, 0, 1, 3)
        back = back.reshape(4 * r_size, rows_two, quarter * q_size)
        back = lax.all_to_all(back, "mom", split_axis=0, concat_axis=1, tiled=True)
        back = back.reshape(rows_one, p_size, 4, quarter, q_size).transpose(0, 2, 3, 1, 4)
        state = source + back.reshape(source.shape)
    return state, component


def solution(mesh):
    spread = ("energy", "mom")
    placed = (P(spread, None, None), P(spread, None)) + (P(),) * 10
    devices = mesh.shape["mom"]

    def body(source, green, *rest):
        whole_rows = source.shape[0] % 4 == 0 and green.shape[0] % 4 == 0
        chosen = shards if whole_rows and source.shape[1] == LANES else shards_by_row
        return chosen(devices, source, green, *rest)

    return jax.shard_map(
        body,
        mesh=mesh,
        in_specs=placed,
        out_specs=(P(spread, None, None), P(spread, None, None)),
        check_vma=False,
    )
```

time: 932 us -> 570 us (0.61)
  local copies, waits for them, and re-layouts: 362 us -> 84.7 us
  blocking collectives: 295 us -> 30.1 us
  Pallas kernels: 0 us -> 213 us
  matrix products: 161 us -> 0 us
  waiting for transfers between devices: 83.5 us -> 163 us
  starting transfers between devices: 6.72 us -> 74.1 us
  other arithmetic: 13.5 us -> 0.1 us
    all_to_all x3 -> x1, blocking collectives: 295 us -> 30.1 us  [exchange(): return lax.all_to_all(sent, 'mom', split_axis=0, concat_axis=0, tiled=True)]
    reshape x20 -> x10, local copies, waits for them, and re-layouts: 271 us -> 22.9 us  [the longest x1 18.7 us: shards(): couple_two.reshape(angles, 4, quarter, 4, quarter, 4)]
    pallas_call x0 -> x27, Pallas kernels: none -> 213 us  [the longest x8 87.4 us: component_one(): pl.pallas_call(functools.partial(one_kernel, g, arrived), grid=(steps,),...]
    dot_general x20 -> x0, matrix products: 161 us -> none  [the longest x8 120 us: interp(): jnp.einsum('rcx,yx->rcy', values, smat, precision=lax.Precision.HIGHEST)]
    all_to_all x1 -> x15, waiting for transfers between devices: 83.5 us -> 163 us  [exchange(): return lax.all_to_all(sent, 'mom', split_axis=0, concat_axis=0, tiled=True)]
    all_to_all x1 -> x15, starting transfers between devices: 6.72 us -> 74.1 us  [exchange(): return lax.all_to_all(sent, 'mom', split_axis=0, concat_axis=0, tiled=True)]
    transpose x4 -> x2, local copies, waits for them, and re-layouts: 74.7 us -> 11.1 us  [the longest x1 11.1 us: shards(): couple_two = couple_two.reshape(angles, 4, quarter, 4, quarter, 4).transp...]
    unnamed x34 -> x108, local copies, waits for them, and re-layouts: 0.07 us -> 47.5 us
  transfers between devices with their start and end apart: 1 -> 15, of which waited for: 1 -> 14; matrix products, arithmetic and copies ran while one was open for 1% -> 6% of each run, Pallas kernels for 0% -> 30%
where the time goes in v1:
time: 570 us; the launch traced here: 566 us
  Pallas kernels  213 us (37%)
  waiting for transfers between devices  163 us (29%)
  local copies, waits for them, and re-layouts  84.7 us (15%)
  starting transfers between devices  74.1 us (13%)
  blocking collectives  30.1 us (5%)
    all_to_all x15, waiting for transfers between devices, exchange(): return lax.all_to_all(sent, 'mom', split_axis=0, concat_axis=0, tiled=True)  163 us
    pallas_call x8, Pallas kernels, component_one(): pl.pallas_call(functools.partial(one_kernel, g, arrived), grid=(steps,),...  87.4 us
    all_to_all x15, starting transfers between devices, exchange(): return lax.all_to_all(sent, 'mom', split_axis=0, concat_axis=0, tiled=True)  74.1 us
    pallas_call x8, Pallas kernels, component_two(): pl.pallas_call(two_kernel, grid=(steps,), in_specs=[pl.BlockSpec(arrived....  72.7 us
    unnamed x108, local copies, waits for them, and re-layouts  47.5 us
    all_to_all x1, blocking collectives, exchange(): return lax.all_to_all(sent, 'mom', split_axis=0, concat_axis=0, tiled=True)  30.1 us
    pallas_call x2, Pallas kernels, spline_maps(): pl.pallas_call(functools.partial(map_kernel, count), grid=(angles, size /...  19.9 us
    reshape x1, local copies, waits for them, and re-layouts, shards(): couple_two.reshape(angles, 4, quarter, 4, quarter, 4)  18.7 us
  transfers between devices with their start and end apart: 15, of which 14 were waited for; matrix products, arithmetic and copies ran while one was open for 6% of the time, Pallas kernels for 30%

profile of v1, /device:TPU:9, one launch (start us, length us, event | category | flops | bytes accessed | tf_op | source)
XLA Modules:
  0.0 566.0 jit_solution(3974965509756977890)
XLA Ops:
  0.7 7.3 %turn_source.1.base_ref = f32[4,2,1024,128]{3,2,1,0:T(8,128)} custom-call(f32[8,128,1024]{2,1,0:T(8,128)} %source_ref.9), custom_call_target="tpu_custom_call" | custom-call | bytes 8388608 | tf_op jit(solution)/shard_map/turn_source/pallas_call | solution.py:92
  9.5 9.9 %spline_maps.2 = (bf16[1024,2048]{1,0:T(8,128)(2,1)}, bf16[1024,2048]{1,0:T(8,128)(2,1)}) custom-call(f32[2,1024,10]{2,1,0:T(8,128)} %copy.42.table_ref), custom_call_target="tpu_custom_call" | custom-call | flops 41943040 | bytes 8388608 | tf_op jit(solution)/shard_map/spline_maps/pallas_call | solution.py:68
  21.6 10.6 %component_one.8 = f32[16,2,2,32,128]{4,3,2,1,0:T(8,128)} custom-call(f32[4,2,1024,128]{3,2,1,0:T(8,128)S(1)} %copy-done, f32[2,4,128,128]{3,2,1,0:T(8,128)S(1)} %copy-done.8, bf16[1024,2048]{1,0:T(8,128)(2,1)} %get-tuple-element.6.refs_1_.refs_5_, bf16[1024,2048]{1,0:T(8,128)(2,1)} %get-tuple-element.7.refs_2_.refs_6_), custom_call_target="tpu_custom_call" | custom-call | flops 4831838208 | bytes 12582912 | tf_op jit(solution)/shard_map/component_one/pallas_call | solution.py:176
  32.2 6.6 %all-to-all-start = ((f32[16,2,64,128]{3,2,1,0:T(8,128)}), f32[16,2,64,128]{3,2,1,0:T(8,128)S(1)}, u32[]{:S(2)}, u32[]{:S(2)}) async-start(f32[16,2,64,128]{3,2,1,0:T(8,128)} %bitcast.4), calls=%async_computation | async-start | bytes 2097152 | tf_op jit(solution)/shard_map/all_to_all | solution.py:343
  40.9 10.6 %component_one.9 = f32[16,2,2,32,128]{4,3,2,1,0:T(8,128)} custom-call(f32[4,2,1024,128]{3,2,1,0:T(8,128)S(1)} %copy-done.1, f32[2,4,128,128]{3,2,1,0:T(8,128)S(1)} %copy-done.8, bf16[1024,2048]{1,0:T(8,128)(2,1)} %get-tuple-element.6.refs_1_.refs_5_, bf16[1024,2048]{1,0:T(8,128)(2,1)} %get-tuple-element.7.refs_2_.refs_6_), custom_call_target="tpu_custom_call" | custom-call | flops 4831838208 | bytes 12582912 | tf_op jit(solution)/shard_map/component_one/pallas_call | solution.py:176
  51.5 12.1 %all-to-all-done.x_ref = f32[16,2,64,128]{3,2,1,0:T(8,128)S(1)} async-done(((f32[16,2,64,128]{3,2,1,0:T(8,128)}), f32[16,2,64,128]{3,2,1,0:T(8,128)S(1)}, u32[]{:S(2)}, u32[]{:S(2)}) %all-to-all-start) | async-done | bytes 1048608 | tf_op jit(solution)/shard_map/all_to_all | solution.py:343
  64.7 4.8 all-to-all-start.2
  71.7 10.6 %component_one.10 = f32[16,2,2,32,128]{4,3,2,1,0:T(8,128)} custom-call(f32[4,2,1024,128]{3,2,1,0:T(8,128)S(1)} %copy-done.2, f32[2,4,128,128]{3,2,1,0:T(8,128)S(1)} %copy-done.8, bf16[1024,2048]{1,0:T(8,128)(2,1)} %get-tuple-element.6.refs_1_.refs_5_, bf16[1024,2048]{1,0:T(8,128)(2,1)} %get-tuple-element.7.refs_2_.refs_6_), custom_call_target="tpu_custom_call" | custom-call | flops 4831838208 | bytes 12582912 | tf_op jit(solution)/shard_map/component_one/pallas_call | solution.py:176
  82.3 12.1 %all-to-all-done.2.x_ref = f32[16,2,64,128]{3,2,1,0:T(8,128)S(1)} async-done(((f32[16,2,64,128]{3,2,1,0:T(8,128)}), f32[16,2,64,128]{3,2,1,0:T(8,128)S(1)}, u32[]{:S(2)}, u32[]{:S(2)}) %all-to-all-start.2) | async-done | bytes 1048608 | tf_op jit(solution)/shard_map/all_to_all | solution.py:343
  102.3 10.6 %component_one.11 = f32[16,2,2,32,128]{4,3,2,1,0:T(8,128)} custom-call(f32[4,2,1024,128]{3,2,1,0:T(8,128)S(1)} %copy-done.3, f32[2,4,128,128]{3,2,1,0:T(8,128)S(1)} %copy-done.8, bf16[1024,2048]{1,0:T(8,128)(2,1)} %get-tuple-element.6.refs_1_.refs_5_, bf16[1024,2048]{1,0:T(8,128)(2,1)} %get-tuple-element.7.refs_2_.refs_6_), custom_call_target="tpu_custom_call" | custom-call | flops 4831838208 | bytes 12582912 | tf_op jit(solution)/shard_map/component_one/pallas_call | solution.py:176
  113.0 12.1 %all-to-all-done.4.x_ref = f32[16,2,64,128]{3,2,1,0:T(8,128)S(1)} async-done(((f32[16,2,64,128]{3,2,1,0:T(8,128)}), f32[16,2,64,128]{3,2,1,0:T(8,128)S(1)}, u32[]{:S(2)}, u32[]{:S(2)}) %all-to-all-start.4) | async-done | bytes 1048608 | tf_op jit(solution)/shard_map/all_to_all | solution.py:343
  126.0 4.8 all-to-all-start.6
  130.8 18.7 %reshape.109 = f32[2,4,32,4,32,4]{5,4,3,2,1,0:T(8,128)} reshape(f32[2,4,128,128]{3,2,1,0:T(8,128)S(1)} %copy-done.44) | data formatting | bytes 1048576 | tf_op jit(solution)/shard_map/reshape | solution.py:380
  149.5 11.1 %copy.43 = f32[2,4,4,32,4,32]{5,4,3,2,1,0:T(4,128)S(1)} copy(f32[2,4,4,32,4,32]{4,5,2,3,1,0:T(8,128)} %bitcast.60) | data formatting | bytes 1048576 | tf_op jit(solution)/shard_map/transpose | solution.py:381
  166.8 10.0 %spline_maps.3 = (bf16[1024,2048]{1,0:T(8,128)(2,1)}, bf16[1024,2048]{1,0:T(8,128)(2,1)}) custom-call(f32[2,1024,10]{2,1,0:T(8,128)} %copy.49.table_ref), custom_call_target="tpu_custom_call" | custom-call | flops 41943040 | bytes 8388608 | tf_op jit(solution)/shard_map/spline_maps/pallas_call | solution.py:68
  179.1 8.5 %component_two.8 = f32[16,2,2,32,128]{4,3,2,1,0:T(8,128)S(1)} custom-call(f32[16,2,64,128]{3,2,1,0:T(8,128)S(1)} %copy-done.29, f32[2,4,128,128]{3,2,1,0:T(8,128)S(1)} %copy-done.34, f32[4,1024,2]{2,1,0:T(8,128)S(1)} %bitcast.48, bf16[1024,2048]{1,0:T(8,128)(2,1)} %get-tuple-element.8.high_ref, bf16[1024,2048]{1,0:T(8,128)(2,1)} %get-tuple-element.9.low_ref), custom_call_target="tpu_custom_call" | custom-call | flops 3623878656 | bytes 9437184 | tf_op jit(solution)/shard_map/component_two/pallas_call | solution.py:236
  189.7 6.0 %all-to-all-start.1 = ((f32[16,2,64,128]{3,2,1,0:T(8,128)}), f32[16,2,64,128]{3,2,1,0:T(8,128)S(1)}, u32[]{:S(2)}, u32[]{:S(2)}) async-start(f32[16,2,64,128]{3,2,1,0:T(8,128)} %bitcast.56), calls=%async_computation.1 | async-start | bytes 2097152 | tf_op jit(solution)/shard_map/all_to_all | solution.py:343
  198.0 8.5 %component_two.9 = f32[16,2,2,32,128]{4,3,2,1,0:T(8,128)S(1)} custom-call(f32[16,2,64,128]{3,2,1,0:T(8,128)S(1)} %copy-done.27, f32[2,4,128,128]{3,2,1,0:T(8,128)S(1)} %copy-done.35, f32[4,1024,2]{2,1,0:T(8,128)S(1)} %bitcast.49, bf16[1024,2048]{1,0:T(8,128)(2,1)} %get-tuple-element.8.high_ref, bf16[1024,2048]{1,0:T(8,128)(2,1)} %get-tuple-element.9.low_ref), custom_call_target="tpu_custom_call" | custom-call | flops 3623878656 | bytes 9437184 | tf_op jit(solution)/shard_map/component_two/pallas_call | solution.py:236
  207.5 13.1 %all-to-all-done.1.refs_0_ = f32[16,2,64,128]{3,2,1,0:T(8,128)S(1)} async-done(((f32[16,2,64,128]{3,2,1,0:T(8,128)}), f32[16,2,64,128]{3,2,1,0:T(8,128)S(1)}, u32[]{:S(2)}, u32[]{:S(2)}) %all-to-all-start.1) | async-done | bytes 1048608 | tf_op jit(solution)/shard_map/all_to_all | solution.py:343
  220.6 4.8 all-to-all-start.3
  229.2 8.5 %component_two.10 = f32[16,2,2,32,128]{4,3,2,1,0:T(8,128)S(1)} custom-call(f32[16,2,64,128]{3,2,1,0:T(8,128)S(1)} %copy-done.25, f32[2,4,128,128]{3,2,1,0:T(8,128)S(1)} %copy-done.36, f32[4,1024,2]{2,1,0:T(8,128)S(1)} %bitcast.50, bf16[1024,2048]{1,0:T(8,128)(2,1)} %get-tuple-element.8.high_ref, bf16[1024,2048]{1,0:T(8,128)(2,1)} %get-tuple-element.9.low_ref), custom_call_target="tpu_custom_call" | custom-call | flops 3623878656 | bytes 9437184 | tf_op jit(solution)/shard_map/component_two/pallas_call | solution.py:236
  238.8 11.5 %all-to-all-done.3.refs_1_ = f32[16,2,64,128]{3,2,1,0:T(8,128)S(1)} async-done(((f32[16,2,64,128]{3,2,1,0:T(8,128)}), f32[16,2,64,128]{3,2,1,0:T(8,128)S(1)}, u32[]{:S(2)}, u32[]{:S(2)}) %all-to-all-start.3) | async-done | bytes 1048608 | tf_op jit(solution)/shard_map/all_to_all | solution.py:343
  250.3 4.8 all-to-all-start.5
  258.9 8.5 %component_two.11 = f32[16,2,2,32,128]{4,3,2,1,0:T(8,128)S(1)} custom-call(f32[16,2,64,128]{3,2,1,0:T(8,128)S(1)} %copy-done.23, f32[2,4,128,128]{3,2,1,0:T(8,128)S(1)} %copy-done.37, f32[4,1024,2]{2,1,0:T(8,128)S(1)} %bitcast.51, bf16[1024,2048]{1,0:T(8,128)(2,1)} %get-tuple-element.8.high_ref, bf16[1024,2048]{1,0:T(8,128)(2,1)} %get-tuple-element.9.low_ref), custom_call_target="tpu_custom_call" | custom-call | flops 3623878656 | bytes 9437184 | tf_op jit(solution)/shard_map/component_two/pallas_call | solution.py:236
  268.5 11.5 %all-to-all-done.5.refs_2_ = f32[16,2,64,128]{3,2,1,0:T(8,128)S(1)} async-done(((f32[16,2,64,128]{3,2,1,0:T(8,128)}), f32[16,2,64,128]{3,2,1,0:T(8,128)S(1)}, u32[]{:S(2)}, u32[]{:S(2)}) %all-to-all-start.5) | async-done | bytes 1048608 | tf_op jit(solution)/shard_map/all_to_all | solution.py:343
  280.0 30.1 %all_to_all.80.refs_3_ = f32[16,2,64,128]{3,2,1,0:T(8,128)S(1)} all-to-all(f32[16,2,64,128]{3,2,1,0:T(8,128)} %bitcast.59), channel_id=1, replica_groups=mesh['energy'=2,'mom'=16] {'mom'}, dimensions={0} | all-to-all | bytes 2097152 | tf_op jit(solution)/shard_map/all_to_all | solution.py:343
  311.2 11.5 %component_one.12 = f32[16,2,2,32,128]{4,3,2,1,0:T(8,128)S(1)} custom-call(f32[4,2,1024,128]{3,2,1,0:T(8,128)} %turn_source.1.base_ref, f32[16,2,64,128]{3,2,1,0:T(8,128)S(1)} %all-to-all-done.1.refs_0_, f32[16,2,64,128]{3,2,1,0:T(8,128)S(1)} %all-to-all-done.3.refs_1_, f32[16,2,64,128]{3,2,1,0:T(8,128)S(1)} %all-to-all-done.5.refs_2_, ...), custom_call_target="tpu_custom_call" | custom-call | flops 4831838208 | bytes 12582912 | tf_op jit(solution)/shard_map/component_one/pallas_call | solution.py:176
  330.3 11.1 %component_one.13 = f32[16,2,2,32,128]{4,3,2,1,0:T(8,128)S(1)} custom-call(f32[4,2,1024,128]{3,2,1,0:T(8,128)} %turn_source.1.base_ref, f32[16,2,64,128]{3,2,1,0:T(8,128)S(1)} %all-to-all-done.1.refs_0_, f32[16,2,64,128]{3,2,1,0:T(8,128)S(1)} %all-to-all-done.3.refs_1_, f32[16,2,64,128]{3,2,1,0:T(8,128)S(1)} %all-to-all-done.5.refs_2_, ...), custom_call_target="tpu_custom_call" | custom-call | flops 4831838208 | bytes 12582912 | tf_op jit(solution)/shard_map/component_one/pallas_call | solution.py:176
  342.4 10.6 %all-to-all-done.8.x_ref = f32[16,2,64,128]{3,2,1,0:T(8,128)} async-done(((f32[16,2,64,128]{3,2,1,0:T(8,128)}), f32[16,2,64,128]{3,2,1,0:T(8,128)}, u32[]{:S(2)}, u32[]{:S(2)}) %all-to-all-start.8) | async-done | bytes 1048608 | tf_op jit(solution)/shard_map/all_to_all | solution.py:343
  353.1 4.8 all-to-all-start.10
  360.1 11.1 %component_one.14 = f32[16,2,2,32,128]{4,3,2,1,0:T(8,128)S(1)} custom-call(f32[4,2,1024,128]{3,2,1,0:T(8,128)} %turn_source.1.base_ref, f32[16,2,64,128]{3,2,1,0:T(8,128)S(1)} %all-to-all-done.1.refs_0_, f32[16,2,64,128]{3,2,1,0:T(8,128)S(1)} %all-to-all-done.3.refs_1_, f32[16,2,64,128]{3,2,1,0:T(8,128)S(1)} %all-to-all-done.5.refs_2_, ...), custom_call_target="tpu_custom_call" | custom-call | flops 4831838208 | bytes 12582912 | tf_op jit(solution)/shard_map/component_one/pallas_call | solution.py:176
  372.2 10.6 %all-to-all-done.10.x_ref = f32[16,2,64,128]{3,2,1,0:T(8,128)} async-done(((f32[16,2,64,128]{3,2,1,0:T(8,128)}), f32[16,2,64,128]{3,2,1,0:T(8,128)}, u32[]{:S(2)}, u32[]{:S(2)}) %all-to-all-start.10) | async-done | bytes 1048608 | tf_op jit(solution)/shard_map/all_to_all | solution.py:343
  382.8 4.8 all-to-all-start.12
  389.9 11.1 %component_one.15 = f32[16,2,2,32,128]{4,3,2,1,0:T(8,128)S(1)} custom-call(f32[4,2,1024,128]{3,2,1,0:T(8,128)} %turn_source.1.base_ref, f32[16,2,64,128]{3,2,1,0:T(8,128)S(1)} %all-to-all-done.1.refs_0_, f32[16,2,64,128]{3,2,1,0:T(8,128)S(1)} %all-to-all-done.3.refs_1_, f32[16,2,64,128]{3,2,1,0:T(8,128)S(1)} %all-to-all-done.5.refs_2_, ...), custom_call_target="tpu_custom_call" | custom-call | flops 4831838208 | bytes 12582912 | tf_op jit(solution)/shard_map/component_one/pallas_call | solution.py:176
  402.0 10.6 %all-to-all-done.12.x_ref = f32[16,2,64,128]{3,2,1,0:T(8,128)} async-done(((f32[16,2,64,128]{3,2,1,0:T(8,128)}), f32[16,2,64,128]{3,2,1,0:T(8,128)}, u32[]{:S(2)}, u32[]{:S(2)}) %all-to-all-start.12) | async-done | bytes 1048608 | tf_op jit(solution)/shard_map/all_to_all | solution.py:343
  412.6 4.8 all-to-all-start.14
  420.0 9.8 %component_two.13.sent_ref = f32[16,2,2,32,128]{4,3,2,1,0:T(8,128)} custom-call(f32[16,2,64,128]{3,2,1,0:T(8,128)} %all-to-all-done.10.x_ref, f32[2,4,128,128]{3,2,1,0:T(8,128)S(1)} %copy-done.38, f32[4,1024,2]{2,1,0:T(8,128)S(1)} %bitcast.52, bf16[1024,2048]{1,0:T(8,128)(2,1)} %get-tuple-element.8.high_ref, bf16[1024,2048]{1,0:T(8,128)(2,1)} %get-tuple-element.9.low_ref), custom_call_target="tpu_custom_call" | custom-call | flops 3623878656 | bytes 9437184 | tf_op jit(solution)/shard_map/component_two/pallas_call | solution.py:236
  429.9 12.4 %all-to-all-done.14.x_ref = f32[16,2,64,128]{3,2,1,0:T(8,128)S(1)} async-done(((f32[16,2,64,128]{3,2,1,0:T(8,128)}), f32[16,2,64,128]{3,2,1,0:T(8,128)S(1)}, u32[]{:S(2)}, u32[]{:S(2)}) %all-to-all-start.14) | async-done | bytes 1048608 | tf_op jit(solution)/shard_map/all_to_all | solution.py:343
  442.3 4.8 all-to-all-start.11
  448.1 9.7 %component_two.14.sent_ref = f32[16,2,2,32,128]{4,3,2,1,0:T(8,128)} custom-call(f32[16,2,64,128]{3,2,1,0:T(8,128)} %all-to-all-done.12.x_ref, f32[2,4,128,128]{3,2,1,0:T(8,128)S(1)} %copy-done.39, f32[4,1024,2]{2,1,0:T(8,128)S(1)} %bitcast.53, bf16[1024,2048]{1,0:T(8,128)(2,1)} %get-tuple-element.8.high_ref, bf16[1024,2048]{1,0:T(8,128)(2,1)} %get-tuple-element.9.low_ref), custom_call_target="tpu_custom_call" | custom-call | flops 3623878656 | bytes 9437184 | tf_op jit(solution)/shard_map/component_two/pallas_call | solution.py:236
  457.8 14.3 %all-to-all-done.11.back_ref = f32[16,2,64,128]{3,2,1,0:T(8,128)} async-done(((f32[16,2,64,128]{3,2,1,0:T(8,128)}), f32[16,2,64,128]{3,2,1,0:T(8,128)}, u32[]{:S(2)}, u32[]{:S(2)}) %all-to-all-start.11) | async-done | bytes 1048608 | tf_op jit(solution)/shard_map/all_to_all | solution.py:343
  472.1 4.8 all-to-all-start.13
  477.9 9.4 %component_two.15.sent_ref = f32[16,2,2,32,128]{4,3,2,1,0:T(8,128)} custom-call(f32[16,2,64,128]{3,2,1,0:T(8,128)S(1)} %all-to-all-done.14.x_ref, f32[2,4,128,128]{3,2,1,0:T(8,128)S(1)} %copy-done.40, f32[4,1024,2]{2,1,0:T(8,128)S(1)} %bitcast.54, bf16[1024,2048]{1,0:T(8,128)(2,1)} %get-tuple-element.8.high_ref, bf16[1024,2048]{1,0:T(8,128)(2,1)} %get-tuple-element.9.low_ref), custom_call_target="tpu_custom_call" | custom-call | flops 3623878656 | bytes 9437184 | tf_op jit(solution)/shard_map/component_two/pallas_call | solution.py:236
  487.3 14.6 %all-to-all-done.13.back_ref = f32[16,2,64,128]{3,2,1,0:T(8,128)} async-done(((f32[16,2,64,128]{3,2,1,0:T(8,128)}), f32[16,2,64,128]{3,2,1,0:T(8,128)}, u32[]{:S(2)}, u32[]{:S(2)}) %all-to-all-start.13) | async-done | bytes 1048608 | tf_op jit(solution)/shard_map/all_to_all | solution.py:343
  501.9 4.8 all-to-all-start.15
  507.7 9.7 %component_two.12.sent_ref = f32[16,2,2,32,128]{4,3,2,1,0:T(8,128)} custom-call(f32[16,2,64,128]{3,2,1,0:T(8,128)} %all-to-all-done.8.x_ref, f32[2,4,128,128]{3,2,1,0:T(8,128)S(1)} %copy-done.41, f32[4,1024,2]{2,1,0:T(8,128)S(1)} %bitcast.55, bf16[1024,2048]{1,0:T(8,128)(2,1)} %get-tuple-element.8.high_ref, bf16[1024,2048]{1,0:T(8,128)(2,1)} %get-tuple-element.9.low_ref), custom_call_target="tpu_custom_call" | custom-call | flops 3623878656 | bytes 9437184 | tf_op jit(solution)/shard_map/component_two/pallas_call | solution.py:236
  517.4 14.2 %all-to-all-done.15.back_ref = f32[16,2,64,128]{3,2,1,0:T(8,128)S(1)} async-done(((f32[16,2,64,128]{3,2,1,0:T(8,128)}), f32[16,2,64,128]{3,2,1,0:T(8,128)S(1)}, u32[]{:S(2)}, u32[]{:S(2)}) %all-to-all-start.15) | async-done | bytes 1048608 | tf_op jit(solution)/shard_map/all_to_all | solution.py:343
  531.6 4.8 all-to-all-start.9
  (143 shorter events, 92.9 us)
Async XLA Ops:
  0.6 7.3 %copy-start.48 = (f32[2,4,1024]{2,1,0:T(4,128)S(1)}, f32[2,4,1024]{2,1,0:T(4,128)}, u32[]{:S(2)}) copy-start(f32[2,4,1024]{2,1,0:T(4,128)} %param.19) | copy-start | bytes 98308
  0.6 7.3 %copy-start.49 = (f32[2,4,1024]{2,1,0:T(4,128)S(1)}, f32[2,4,1024]{2,1,0:T(4,128)}, u32[]{:S(2)}) copy-start(f32[2,4,1024]{2,1,0:T(4,128)} %param.18) | copy-start | bytes 98308
  0.7 7.4 %copy-start.52 = (s32[2,1024]{1,0:T(2,128)S(1)}, s32[2,1024]{1,0:T(2,128)}, u32[]{:S(2)}) copy-start(s32[2,1024]{1,0:T(2,128)} %param.17) | copy-start | bytes 24580
  0.7 7.4 %copy-start.53 = (s32[2,1024]{1,0:T(2,128)S(1)}, s32[2,1024]{1,0:T(2,128)}, u32[]{:S(2)}) copy-start(s32[2,1024]{1,0:T(2,128)} %param.16) | copy-start | bytes 24580
  0.7 18.7 %copy-start.8 = (f32[2,4,128,128]{3,2,1,0:T(8,128)S(1)}, f32[2,4,128,128]{3,2,1,0:T(8,128)}, u32[]{:S(2)}) copy-start(f32[2,4,128,128]{3,2,1,0:T(8,128)} %refs_4_.7) | copy-start | bytes 1572868
  19.4 2.2 copy-start
  32.2 31.5 %all-to-all-start = ((f32[16,2,64,128]{3,2,1,0:T(8,128)}), f32[16,2,64,128]{3,2,1,0:T(8,128)S(1)}, u32[]{:S(2)}, u32[]{:S(2)}) async-start(f32[16,2,64,128]{3,2,1,0:T(8,128)} %bitcast.4), calls=%async_computation | async-start | bytes 2097152 | tf_op jit(solution)/shard_map/all_to_all | solution.py:343
  38.7 2.2 copy-start.1
  63.7 1.1 copy-start.28
  64.7 29.7 %all-to-all-start.2 = ((f32[16,2,64,128]{3,2,1,0:T(8,128)}), f32[16,2,64,128]{3,2,1,0:T(8,128)S(1)}, u32[]{:S(2)}, u32[]{:S(2)}) async-start(f32[16,2,64,128]{3,2,1,0:T(8,128)} %bitcast.15), calls=%async_computation.2 | async-start | bytes 2097152 | tf_op jit(solution)/shard_map/all_to_all | solution.py:343
  69.5 2.2 copy-start.2
  95.4 29.7 %all-to-all-start.4 = ((f32[16,2,64,128]{3,2,1,0:T(8,128)}), f32[16,2,64,128]{3,2,1,0:T(8,128)S(1)}, u32[]{:S(2)}, u32[]{:S(2)}) async-start(f32[16,2,64,128]{3,2,1,0:T(8,128)} %bitcast.18), calls=%async_computation.4 | async-start | bytes 2097152 | tf_op jit(solution)/shard_map/all_to_all | solution.py:343
  100.1 2.2 copy-start.3
  102.3 28.5 %copy-start.44 = (f32[2,4,128,128]{3,2,1,0:T(8,128)S(1)}, f32[2,4,128,128]{3,2,1,0:T(8,128)}, u32[]{:S(2)}) copy-start(f32[2,4,128,128]{3,2,1,0:T(8,128)} %param.15) | copy-start | bytes 1572868
  126.0 62.7 %all-to-all-start.6 = ((f32[16,2,64,128]{3,2,1,0:T(8,128)}), f32[16,2,64,128]{3,2,1,0:T(8,128)S(1)}, u32[]{:S(2)}, u32[]{:S(2)}) async-start(f32[16,2,64,128]{3,2,1,0:T(8,128)} %bitcast.20), calls=%async_computation.6 | async-start | bytes 2097152 | tf_op jit(solution)/shard_map/all_to_all | solution.py:343
  149.5 12.8 %copy-start.45 = (f32[8,1024]{1,0:T(8,128)S(1)}, f32[8,1024]{1,0:T(8,128)}, u32[]{:S(2)}) copy-start(f32[8,1024]{1,0:T(8,128)} %param.13) | copy-start | bytes 98308
  160.5 3.6 copy-start.46
  160.5 4.0 copy-start.47
  160.5 4.3 copy-start.50
  160.6 4.6 copy-start.51
  164.2 31.5 %copy-start.17 = (f32[2,4,32,32]{0,2,3,1:T(8,128)}, f32[2,4,32,32]{0,2,3,1:T(8,128)S(1)}, u32[]{:S(2)}) copy-start(f32[2,4,32,32]{0,2,3,1:T(8,128)S(1)} %copy.44) | copy-start | bytes 98308
  176.8 1.2 copy-start.29
  187.6 1.1 copy-start.30
  189.7 30.9 %all-to-all-start.1 = ((f32[16,2,64,128]{3,2,1,0:T(8,128)}), f32[16,2,64,128]{3,2,1,0:T(8,128)S(1)}, u32[]{:S(2)}, u32[]{:S(2)}) async-start(f32[16,2,64,128]{3,2,1,0:T(8,128)} %bitcast.56), calls=%async_computation.1 | async-start | bytes 2097152 | tf_op jit(solution)/shard_map/all_to_all | solution.py:343
  195.7 1.2 copy-start.27
  220.6 29.7 %all-to-all-start.3 = ((f32[16,2,64,128]{3,2,1,0:T(8,128)}), f32[16,2,64,128]{3,2,1,0:T(8,128)S(1)}, u32[]{:S(2)}, u32[]{:S(2)}) async-start(f32[16,2,64,128]{3,2,1,0:T(8,128)} %bitcast.57), calls=%async_computation.3 | async-start | bytes 2097152 | tf_op jit(solution)/shard_map/all_to_all | solution.py:343
  225.4 1.6 copy-start.18
  227.0 1.2 copy-start.25
  250.3 29.7 %all-to-all-start.5 = ((f32[16,2,64,128]{3,2,1,0:T(8,128)}), f32[16,2,64,128]{3,2,1,0:T(8,128)S(1)}, u32[]{:S(2)}, u32[]{:S(2)}) async-start(f32[16,2,64,128]{3,2,1,0:T(8,128)} %bitcast.58), calls=%async_computation.5 | async-start | bytes 2097152 | tf_op jit(solution)/shard_map/all_to_all | solution.py:343
  255.1 1.6 copy-start.19
  256.7 1.2 copy-start.23
  310.1 1.0 copy-start.9
  311.1 11.5 %copy-start.4 = (f32[16,2,64,128]{3,2,1,0:T(8,128)}, f32[16,2,64,128]{3,2,1,0:T(8,128)S(1)}, u32[]{:S(2)}) copy-start(f32[16,2,64,128]{3,2,1,0:T(8,128)S(1)} %all_to_all.80.refs_3_) | copy-start | bytes 3145732
  323.7 29.4 %all-to-all-start.8 = ((f32[16,2,64,128]{3,2,1,0:T(8,128)}), f32[16,2,64,128]{3,2,1,0:T(8,128)}, u32[]{:S(2)}, u32[]{:S(2)}) async-start(f32[16,2,64,128]{3,2,1,0:T(8,128)} %bitcast.47), calls=%async_computation.8 | async-start | bytes 2097152 | tf_op jit(solution)/shard_map/all_to_all | solution.py:343
  328.0 1.2 copy-start.5
  353.1 29.8 %all-to-all-start.10 = ((f32[16,2,64,128]{3,2,1,0:T(8,128)}), f32[16,2,64,128]{3,2,1,0:T(8,128)}, u32[]{:S(2)}, u32[]{:S(2)}) async-start(f32[16,2,64,128]{3,2,1,0:T(8,128)} %bitcast.46), calls=%async_computation.10 | async-start | bytes 2097152 | tf_op jit(solution)/shard_map/all_to_all | solution.py:343
  357.8 1.2 copy-start.6
  382.8 29.8 %all-to-all-start.12 = ((f32[16,2,64,128]{3,2,1,0:T(8,128)}), f32[16,2,64,128]{3,2,1,0:T(8,128)}, u32[]{:S(2)}, u32[]{:S(2)}) async-start(f32[16,2,64,128]{3,2,1,0:T(8,128)} %bitcast.45), calls=%async_computation.12 | async-start | bytes 2097152 | tf_op jit(solution)/shard_map/all_to_all | solution.py:343
  387.6 1.2 copy-start.7
  412.6 29.7 %all-to-all-start.14 = ((f32[16,2,64,128]{3,2,1,0:T(8,128)}), f32[16,2,64,128]{3,2,1,0:T(8,128)S(1)}, u32[]{:S(2)}, u32[]{:S(2)}) async-start(f32[16,2,64,128]{3,2,1,0:T(8,128)} %bitcast.44), calls=%async_computation.14 | async-start | bytes 2097152 | tf_op jit(solution)/shard_map/all_to_all | solution.py:343
  417.4 1.6 copy-start.20
  420.0 27.1 %copy-start.21 = (f32[2,4,32,32]{0,2,3,1:T(8,128)S(1)}, f32[2,4,32,32]{0,2,3,1:T(8,128)}, u32[]{:S(2)}) copy-start(f32[2,4,32,32]{0,2,3,1:T(8,128)} %copy-done.17) | copy-start | bytes 98308
  442.3 29.8 %all-to-all-start.11 = ((f32[16,2,64,128]{3,2,1,0:T(8,128)}), f32[16,2,64,128]{3,2,1,0:T(8,128)}, u32[]{:S(2)}, u32[]{:S(2)}) async-start(f32[16,2,64,128]{3,2,1,0:T(8,128)} %bitcast.25), calls=%async_computation.11 | async-start | bytes 2097152 | tf_op jit(solution)/shard_map/all_to_all | solution.py:343
  447.1 1.0 copy-start.39
  472.1 29.8 %all-to-all-start.13 = ((f32[16,2,64,128]{3,2,1,0:T(8,128)}), f32[16,2,64,128]{3,2,1,0:T(8,128)}, u32[]{:S(2)}, u32[]{:S(2)}) async-start(f32[16,2,64,128]{3,2,1,0:T(8,128)} %bitcast.27), calls=%async_computation.13 | async-start | bytes 2097152 | tf_op jit(solution)/shard_map/all_to_all | solution.py:343
  501.9 29.7 %all-to-all-start.15 = ((f32[16,2,64,128]{3,2,1,0:T(8,128)}), f32[16,2,64,128]{3,2,1,0:T(8,128)S(1)}, u32[]{:S(2)}, u32[]{:S(2)}) async-start(f32[16,2,64,128]{3,2,1,0:T(8,128)} %bitcast.29), calls=%async_computation.15 | async-start | bytes 2097152 | tf_op jit(solution)/shard_map/all_to_all | solution.py:343
  531.6 10.0 %copy-start.42 = (f32[16,2,64,128]{3,2,1,0:T(8,128)}, f32[16,2,64,128]{3,2,1,0:T(8,128)S(1)}, u32[]{:S(2)}) copy-start(f32[16,2,64,128]{3,2,1,0:T(8,128)S(1)} %all-to-all-done.15.back_ref) | copy-start | bytes 3145732
  531.6 29.7 %all-to-all-start.9 = ((f32[16,2,64,128]{3,2,1,0:T(8,128)}), f32[16,2,64,128]{3,2,1,0:T(8,128)S(1)}, u32[]{:S(2)}, u32[]{:S(2)}) async-start(f32[16,2,64,128]{3,2,1,0:T(8,128)} %bitcast.23), calls=%async_computation.9 | async-start | bytes 2097152 | tf_op jit(solution)/shard_map/all_to_all | solution.py:343
  (21 other events, 21.3 us)

commit v2 on v1

v2 whole, which is shorter than its diff:
```python
import functools

import jax
import jax.numpy as jnp
from jax import lax
from jax.experimental import pallas as pl
from jax.experimental.pallas import tpu as pltpu
from jax.sharding import PartitionSpec as P

ITERS = 2
LANES = 128
F32 = jnp.float32
BF16 = jnp.bfloat16
VMEM_LIMIT = 60 << 20


def split(value):
    high = value.astype(BF16)
    return high, (value - high.astype(F32)).astype(BF16)


def dot(a, b):
    return jnp.dot(a, b, preferred_element_type=F32)


def dot_nt(a, b):
    return lax.dot_general(a, b, (((1,), (1,)), ((), ())), preferred_element_type=F32)


def call(kernel, name, flops, moved, **kwargs):
    return pl.pallas_call(
        kernel,
        compiler_params=pltpu.CompilerParams(vmem_limit_bytes=VMEM_LIMIT),
        cost_estimate=pl.CostEstimate(flops=flops, bytes_accessed=moved, transcendentals=0),
        name=name,
        **kwargs,
    )


def map_kernel(count, table_ref, high_ref, low_ref):
    table = table_ref[0]
    rows = table.shape[0]
    columns = high_ref.shape[1]
    lane = lax.broadcasted_iota(jnp.int32, (rows, LANES), 1)

    def factor(index, base):
        grid = index.astype(F32) - table[:, base : base + 1]
        total = jnp.zeros((rows, LANES), F32)
        for offset in range(4):
            column = 2 + 4 * base + offset
            total = jnp.where(grid == offset, table[:, column : column + 1], total)
        return total

    first = factor(lane, 0)
    second = factor(lax.rem(lane, count), 1)
    for tile in range(columns // LANES):
        index = lax.div(lane + tile * LANES, count)
        value = jnp.take_along_axis(first, index, axis=1) * second
        high, low = split(value)
        high_ref[:, tile * LANES : (tile + 1) * LANES] = high
        low_ref[:, tile * LANES : (tile + 1) * LANES] = low


def spline_maps(first, second, first_weight, second_weight, count):
    angles, size = first.shape
    table = jnp.concatenate(
        [
            first[..., None].astype(F32),
            second[..., None].astype(F32),
            first_weight.transpose(0, 2, 1),
            second_weight.transpose(0, 2, 1),
        ],
        axis=-1,
    )
    tile = min(256, size)
    out = jax.ShapeDtypeStruct((size, angles * size), BF16)
    spec = pl.BlockSpec((tile, size), lambda k, i: (i, k))
    return call(
        functools.partial(map_kernel, count),
        "spline_maps",
        10 * angles * size * size,
        4 * angles * size * size,
        grid=(angles, size // tile),
        in_specs=[pl.BlockSpec((1, tile, table.shape[2]), lambda k, i: (k, i, 0))],
        out_specs=[spec, spec],
        out_shape=[out, out],
    )(table)


def interpolate(high_ref, low_ref, mixed_high, mixed_low, product):
    high = high_ref[...]
    return (
        product(high, mixed_high[...])
        + product(high, mixed_low[...])
        + product(low_ref[...], mixed_high[...])
    )


def spread_out(value, out_ref, scale_ref=None):
    parts, blocks, near, local, count, channels = out_ref.shape
    for b in range(blocks):
        for n in range(local):
            at = b * local + n
            block = value[:, at * channels : (at + 1) * channels]
            if scale_ref is not None:
                block = block * scale_ref[:, at : at + 1]
            out_ref[:, b, :, n, :, :] = block.reshape(parts, near, count, channels)


def first_kernel(blocks, steps, local, source_ref, couple_ref, high_ref, low_ref, out_ref, m_high, m_low):
    angles, channels, _ = couple_ref.shape
    quarter = channels // 4
    size = source_ref.shape[1]
    i = pl.program_id(0)

    @pl.when(i < steps)
    def _():
        rows = [
            couple_ref[k, g * quarter : (g + 1) * quarter, :] for k in range(angles) for g in blocks
        ]
        w_high, w_low = split(jnp.concatenate(rows, axis=0))
        high, low = split(source_ref[...])
        high, low = split(dot(w_high, high) + dot(w_low, high) + dot(w_high, low))
        r, c = lax.div(i, 4), lax.rem(i, 4)
        for k in range(angles):
            for b in range(len(blocks)):
                at = (k * len(blocks) + b) * quarter
                to = pl.multiple_of((b * local + r) * channels + c * quarter, quarter)
                m_high[pl.ds(to, quarter), k * size : (k + 1) * size] = high[at : at + quarter]
                m_low[pl.ds(to, quarter), k * size : (k + 1) * size] = low[at : at + quarter]

    @pl.when(i >= steps)
    def _():
        spread_out(interpolate(high_ref, low_ref, m_high, m_low, dot_nt), out_ref)


def first_one(blocks, source, couple, maps, near, devices):
    rows, channels, size = source.shape
    local = rows // 4
    angles = couple.shape[0]
    tiles = 4
    out = (devices, len(blocks), near, local, size // (devices * near), channels)
    wide = len(blocks) * local * channels

    def tile(i):
        return jnp.maximum(i - rows, 0)

    return call(
        functools.partial(first_kernel, blocks, rows, local),
        "component_one_first",
        6 * wide * angles * size * (size + channels),
        4 * source.size + 4 * angles * size * size,
        grid=(rows + tiles,),
        in_specs=[
            pl.BlockSpec((None, channels, size), lambda i: (jnp.minimum(i, rows - 1), 0, 0)),
            pl.BlockSpec((angles, None, channels, channels), lambda i: (0, lax.rem(i, 4), 0, 0)),
        ]
        + [pl.BlockSpec((size // tiles, angles * size), lambda i: (tile(i), 0))] * 2,
        out_specs=pl.BlockSpec((devices // tiles,) + out[1:], lambda i: (tile(i), 0, 0, 0, 0, 0)),
        out_shape=jax.ShapeDtypeStruct(out, F32),
        scratch_shapes=[pltpu.VMEM((wide, angles * size), BF16)] * 2,
    )(source, couple, *maps)


def later_kernel(blocks, steps, arrived, *refs):
    backs = refs[:arrived]
    couple_ref, high_ref, low_ref, out_ref, w_high, w_low, m_high, m_low = refs[arrived:]
    angles, _, channels, _ = couple_ref.shape
    quarter = channels // 4
    parts, _, local, per, _ = backs[0].shape
    tile = parts * per
    size = tile * steps
    i = pl.program_id(0)

    @pl.when(i == 0)
    def _():
        lane = lax.broadcasted_iota(jnp.int32, (quarter, channels), 1)
        for k in range(angles):
            for b, g in enumerate(blocks):
                for c in range(4):
                    rows = couple_ref[k, c, g * quarter : (g + 1) * quarter, :]
                    at = (k * len(blocks) + b) * channels + c * quarter
                    inside = lax.div(lane, quarter) == c
                    for other in range(4):
                        shift = ((c - other) * quarter) % channels
                        moved = pltpu.roll(rows, shift, 1) if shift else rows
                        high, low = split(jnp.where(inside, moved, 0.0))
                        lanes = slice(other * channels, (other + 1) * channels)
                        w_high[at : at + quarter, lanes] = high
                        w_low[at : at + quarter, lanes] = low

    @pl.when(i < steps)
    def _():
        for r in range(local):
            pieces = [
                back[:, b, r].reshape(tile, channels)
                for back in backs
                for b in range(back.shape[1])
            ]
            high, low = split(jnp.concatenate(pieces, axis=1))
            mixed = dot_nt(high, w_high[...]) + dot_nt(low, w_high[...]) + dot_nt(high, w_low[...])
            high, low = split(mixed)
            for k in range(angles):
                rows = pl.ds(pl.multiple_of(k * size + i * tile, tile), tile)
                for b in range(len(blocks)):
                    at = (k * len(blocks) + b) * channels
                    to = (b * local + r) * channels
                    m_high[rows, to : to + channels] = high[:, at : at + channels]
                    m_low[rows, to : to + channels] = low[:, at : at + channels]

    @pl.when(i >= steps)
    def _():
        spread_out(interpolate(high_ref, low_ref, m_high, m_low, dot), out_ref)


def later_one(blocks, backs, couple, maps, near):
    devices, _, local, per, channels = backs[0].shape
    size = devices * per
    angles = couple.shape[0]
    steps = tiles = 4
    out = (devices, len(blocks), near, local, size // (devices * near), channels)
    wide = len(blocks) * local * channels

    def tile(i):
        return jnp.maximum(i - steps, 0)

    def step(i):
        return jnp.minimum(i, steps - 1)

    return call(
        functools.partial(later_kernel, blocks, steps, len(backs)),
        "component_one_later",
        6 * wide * angles * size * (size + 4 * channels),
        4 * sum(back.size for back in backs) + 4 * angles * size * size,
        grid=(steps + tiles,),
        in_specs=[
            pl.BlockSpec((devices // steps,) + back.shape[1:], lambda i: (step(i), 0, 0, 0, 0))
            for back in backs
        ]
        + [pl.BlockSpec(couple.shape, lambda i: (0, 0, 0, 0))]
        + [pl.BlockSpec((size // tiles, angles * size), lambda i: (tile(i), 0))] * 2,
        out_specs=pl.BlockSpec((devices // tiles,) + out[1:], lambda i: (tile(i), 0, 0, 0, 0, 0)),
        out_shape=jax.ShapeDtypeStruct(out, F32),
        scratch_shapes=[pltpu.VMEM((angles * len(blocks) * channels, 4 * channels), BF16)] * 2
        + [pltpu.VMEM((angles * size, wide), BF16)] * 2,
    )(*backs, couple, *maps)


def two_kernel(blocks, steps, arrived, *refs):
    values = refs[:arrived]
    couple_ref, green_ref, high_ref, low_ref, out_ref = refs[arrived : arrived + 5]
    turned, w_high, w_low, m_high, m_low = refs[arrived + 5 :]
    angles, _, channels, _ = couple_ref.shape
    quarter = channels // 4
    parts, _, local, per, _ = values[0].shape
    tile = parts * per
    size = tile * steps
    i = pl.program_id(0)

    @pl.when(i == 0)
    def _():
        for k in range(angles):
            for b, g in enumerate(blocks):
                at = k * len(blocks) + b
                rows = [couple_ref[k, g, pl.ds(c, quarter, stride=4), :] for c in range(4)]
                turned[at] = jnp.concatenate(rows, axis=0).T
                rows = [turned[at, pl.ds(c, quarter, stride=4), :] for c in range(4)]
                high, low = split(jnp.concatenate(rows, axis=0))
                w_high[b, :, k * channels : (k + 1) * channels] = high
                w_low[b, :, k * channels : (k + 1) * channels] = low

    @pl.when(i < steps)
    def _():
        for b in range(len(blocks)):
            for p in range(local):
                value = values[0][:, b, p]
                for other in values[1:]:
                    value = value + other[:, b, p]
                high, low = split(value.reshape(tile, channels))
                mixed = dot(high, w_high[b]) + dot(low, w_high[b]) + dot(high, w_low[b])
                high, low = split(mixed)
                to = (b * local + p) * channels
                for k in range(angles):
                    rows = pl.ds(pl.multiple_of(k * size + i * tile, tile), tile)
                    lanes = slice(k * channels, (k + 1) * channels)
                    m_high[rows, to : to + channels] = high[:, lanes]
                    m_low[rows, to : to + channels] = low[:, lanes]

    @pl.when(i >= steps)
    def _():
        spread_out(interpolate(high_ref, low_ref, m_high, m_low, dot), out_ref, green_ref)


def component_two(blocks, values, couple, green, maps, near):
    devices, _, local, per, channels = values[0].shape
    size = devices * per
    angles = couple.shape[0]
    steps = tiles = 4
    out = (devices, len(blocks), near, local, per // near, channels)
    wide = len(blocks) * local * channels

    def tile(i):
        return jnp.maximum(i - steps, 0)

    def step(i):
        return jnp.minimum(i, steps - 1)

    return call(
        functools.partial(two_kernel, blocks, steps, len(values)),
        "component_two",
        6 * wide * angles * size * (size + channels),
        4 * len(values) * values[0].size + 4 * angles * size * size,
        grid=(steps + tiles,),
        in_specs=[
            pl.BlockSpec((devices // steps,) + value.shape[1:], lambda i: (step(i), 0, 0, 0, 0))
            for value in values
        ]
        + [
            pl.BlockSpec(couple.shape, lambda i: (0, 0, 0, 0)),
            pl.BlockSpec((size // tiles, green.shape[1]), lambda i: (tile(i), 0)),
        ]
        + [pl.BlockSpec((size // tiles, angles * size), lambda i: (tile(i), 0))] * 2,
        out_specs=pl.BlockSpec((devices // tiles,) + out[1:], lambda i: (tile(i), 0, 0, 0, 0, 0)),
        out_shape=jax.ShapeDtypeStruct(out, F32),
        scratch_shapes=[pltpu.VMEM((angles * len(blocks), channels, channels), F32)]
        + [pltpu.VMEM((len(blocks), channels, angles * channels), BF16)] * 2
        + [pltpu.VMEM((angles * size, wide), BF16)] * 2,
    )(*values, couple, green, *maps)


def amplitude_kernel(quarter, source_ref, back_ref, *refs):
    out_ref = refs[-1]
    back = back_ref[...]
    turned = back.reshape(-1, back.shape[-1]).T
    for c in range(4):
        out_ref[c] = source_ref[c] + turned[c * quarter : (c + 1) * quarter]


def amplitude_chunk(blocks, source, back, so_far):
    rows, channels, size = source.shape
    devices, _, local, per, _ = back.shape
    quarter = channels // 4
    tile = min(512, size)
    spec = pl.BlockSpec((4, quarter, tile), lambda b, r, i: (r, blocks[0] + b, i))
    in_specs = [
        spec,
        pl.BlockSpec((tile // per, None, None, per, channels), lambda b, r, i: (i, b, r, 0, 0)),
    ]
    args = [source, back]
    aliases = {}
    if so_far is not None:
        in_specs.append(pl.BlockSpec(memory_space=pl.ANY))
        args.append(so_far)
        aliases = {2: 0}
    return call(
        functools.partial(amplitude_kernel, quarter),
        "amplitude",
        back.size,
        12 * back.size,
        grid=(len(blocks), local, size // tile),
        in_specs=in_specs,
        out_specs=spec,
        out_shape=jax.ShapeDtypeStruct(source.shape, F32),
        input_output_aliases=aliases,
    )(*args)


def output_kernel(quarter, sent_ref, *refs):
    out_ref, turned_ref = refs[-2:]
    devices, near, count, channels = sent_ref.shape
    per_tile = LANES // (devices * near)
    for tile in range(count // per_tile):
        rows = [
            sent_ref[:, :, tile * per_tile + i, :].reshape(devices * near, channels)
            for i in range(per_tile)
        ]
        turned = jnp.concatenate(rows, axis=0).T
        for c in range(4):
            turned_ref[tile, pl.ds(c, quarter, stride=4), :] = turned[
                c * quarter : (c + 1) * quarter
            ]
        out_ref[:, tile * LANES : (tile + 1) * LANES] = turned_ref[tile]


def component_chunk(blocks, sent, so_far):
    devices, _, near, local, count, channels = sent.shape
    size = devices * near * count
    in_specs = [
        pl.BlockSpec(
            (devices, None, near, None, count, channels), lambda b, p: (0, b, 0, p, 0, 0)
        )
    ]
    args = [sent]
    aliases = {}
    if so_far is not None:
        in_specs.append(pl.BlockSpec(memory_space=pl.ANY))
        args.append(so_far)
        aliases = {1: 0}
    return call(
        functools.partial(output_kernel, channels // 4),
        "component_out",
        0,
        8 * sent.size,
        grid=(len(blocks), local),
        in_specs=in_specs,
        out_specs=pl.BlockSpec(
            (None, channels, size), lambda b, p: (4 * p + blocks[0] + b, 0, 0)
        ),
        out_shape=jax.ShapeDtypeStruct((4 * local, channels, size), F32),
        scratch_shapes=[pltpu.VMEM((size // LANES, channels, LANES), F32)],
        input_output_aliases=aliases,
    )(*args)


def exchange(values):
    devices, blocks, near, local, count, channels = values.shape
    sent = values.reshape(devices, blocks, near, local * count, channels)
    return lax.all_to_all(sent, "mom", split_axis=0, concat_axis=0, tiled=True)


CHUNKS = ((0,), (1, 2, 3))


def shards(
    devices,
    source,
    green,
    couple_one,
    couple_two,
    p_bracket,
    q_bracket,
    p_weight,
    q_weight,
    qr_bracket,
    r_bracket,
    qr_weight,
    r_weight,
):
    rows_one, channels, size_one = source.shape
    rows_two, size_two = green.shape
    near_r, near_p = rows_one // 4, rows_two // 4
    r_size, p_size = devices * near_r, devices * near_p
    q_size = size_one // p_size

    first_maps = spline_maps(p_bracket, q_bracket, p_weight, q_weight, q_size)

    def by_r(array):
        lead = array.shape[:-1]
        return array.reshape(lead + (q_size, r_size)).swapaxes(-1, -2).reshape(lead + (-1,))

    second_maps = spline_maps(
        by_r(r_bracket), by_r(qr_bracket), by_r(r_weight), by_r(qr_weight), q_size
    )
    green = green.reshape(near_p, 4, q_size, r_size).transpose(3, 2, 1, 0)
    green = green.reshape(size_two, 4 * near_p)
    arrived = []
    for step in range(ITERS):
        if step == 0:
            ones = [
                first_one(blocks, source, couple_one, first_maps, near_p, devices)
                for blocks in CHUNKS
            ]
        else:
            ones = [later_one(blocks, backs, couple_one, first_maps, near_p) for blocks in CHUNKS]
        arrived.append([exchange(one) for one in ones])
        values = [arrived[0]] + ([arrived[step]] if step else [])
        twos = []
        for n, blocks in enumerate(CHUNKS):
            lanes = slice(blocks[0] * near_p, (blocks[-1] + 1) * near_p)
            twos.append(
                component_two(
                    blocks,
                    [value[n] for value in values],
                    couple_two,
                    green[:, lanes],
                    second_maps,
                    near_r,
                )
            )
        backs = [exchange(two) for two in twos]
    component = amplitude = None
    for blocks, two in zip(CHUNKS, twos):
        component = component_chunk(blocks, two, component)
    for blocks, back in zip(CHUNKS, backs):
        amplitude = amplitude_chunk(blocks, source, back, amplitude)
    return amplitude, component


def whole_map(first, second, first_weight, second_weight, first_count, second_count):
    first_rows = jnp.zeros((first.shape[0], first_count), F32)
    second_rows = jnp.zeros((second.shape[0], second_count), F32)
    first_grid = jnp.arange(first_count, dtype=jnp.int32)[None, :] - first[:, None]
    second_grid = jnp.arange(second_count, dtype=jnp.int32)[None, :] - second[:, None]
    for offset in range(4):
        first_rows += jnp.where(first_grid == offset, first_weight[offset][:, None], 0.0)
        second_rows += jnp.where(second_grid == offset, second_weight[offset][:, None], 0.0)
    return (first_rows[:, :, None] * second_rows[:, None, :]).reshape(first.shape[0], -1)


def row_mats(couple, rows, start):
    select = jax.nn.one_hot((start + jnp.arange(rows, dtype=jnp.int32)) % 4, 4, dtype=F32)
    return jnp.einsum("rc,kcmn->krmn", select, couple, precision=lax.Precision.HIGHEST)


def mix_rows(mats, values):
    return jnp.einsum("rmn,rnx->rmx", mats, values, precision=lax.Precision.HIGHEST)


def interpolate_rows(values, matrix):
    return jnp.einsum("rcx,yx->rcy", values, matrix, precision=lax.Precision.HIGHEST)


def shards_by_row(
    devices,
    source,
    green,
    couple_one,
    couple_two,
    p_bracket,
    q_bracket,
    p_weight,
    q_weight,
    qr_bracket,
    r_bracket,
    qr_weight,
    r_weight,
):
    rows_one, channels, size_one = source.shape
    rows_two, size_two = green.shape
    angles = couple_one.shape[0]
    quarter = channels // 4
    r_size, p_size = devices * rows_one // 4, devices * rows_two // 4
    q_size = size_one // p_size
    here = lax.axis_index("mom")
    first = [
        whole_map(p_bracket[k], q_bracket[k], p_weight[k], q_weight[k], p_size, q_size)
        for k in range(angles)
    ]
    second = [
        whole_map(qr_bracket[k], r_bracket[k], qr_weight[k], r_weight[k], q_size, r_size)
        for k in range(angles)
    ]
    mats_one = row_mats(couple_one, rows_one, here * rows_one)
    mats_two = row_mats(couple_two, rows_two, here * rows_two)
    state = source
    for step in range(ITERS):
        one = sum(interpolate_rows(mix_rows(mats_one[k], state), first[k]) for k in range(angles))
        sent = one.reshape(rows_one, 4, quarter, p_size, q_size).transpose(3, 1, 0, 2, 4)
        sent = sent.reshape(4 * p_size, rows_one, quarter * q_size)
        sent = lax.all_to_all(sent, "mom", split_axis=0, concat_axis=1, tiled=True)
        sent = sent.reshape(rows_two, r_size, 4, quarter, q_size).transpose(0, 3, 2, 4, 1)
        sent = sent.reshape(rows_two, channels, size_two)
        total = sum(mix_rows(mats_two[k], interpolate_rows(sent, second[k])) for k in range(angles))
        component = green[:, None, :] * total
        back = component.reshape(rows_two, quarter, 4, q_size, r_size).transpose(4, 2, 0, 1, 3)
        back = back.reshape(4 * r_size, rows_two, quarter * q_size)
        back = lax.all_to_all(back, "mom", split_axis=0, concat_axis=1, tiled=True)
        back = back.reshape(rows_one, p_size, 4, quarter, q_size).transpose(0, 2, 3, 1, 4)
        state = source + back.reshape(source.shape)
    return state, component


def solution(mesh):
    spread = ("energy", "mom")
    placed = (P(spread, None, None), P(spread, None)) + (P(),) * 10
    devices = mesh.shape["mom"]

    def body(source, green, *rest):
        whole_rows = source.shape[0] % 4 == 0 and green.shape[0] % 4 == 0
        chosen = shards if whole_rows and source.shape[1] == LANES else shards_by_row
        return chosen(devices, source, green, *rest)

    return jax.shard_map(
        body,
        mesh=mesh,
        in_specs=placed,
        out_specs=(P(spread, None, None), P(spread, None, None)),
        check_vma=False,
    )
```

time: 570 us -> 475 us (0.83)
  local copies, waits for them, and re-layouts: 84.7 us -> 13.4 us
  Pallas kernels: 213 us -> 162 us
  blocking collectives: 30.1 us -> 75.2 us
  starting transfers between devices: 74.1 us -> 39.3 us
  waiting for transfers between devices: 163 us -> 179 us
    pallas_call x27 -> x14, Pallas kernels: 213 us -> 162 us  [the longest x4 57.5 us: component_two(): call(functools.partial(two_kernel, blocks, steps, len(values)), 'componen...]
    all_to_all x1, blocking collectives: 30.1 us -> 75.2 us  [exchange(): return lax.all_to_all(sent, 'mom', split_axis=0, concat_axis=0, tiled=True)]
    unnamed x108 -> x24, local copies, waits for them, and re-layouts: 47.5 us -> 8.35 us
    all_to_all x15 -> x7, starting transfers between devices: 74.1 us -> 39.3 us  [exchange(): return lax.all_to_all(sent, 'mom', split_axis=0, concat_axis=0, tiled=True)]
    reshape x4 -> x3, local copies, waits for them, and re-layouts: 22.2 us -> 0.3 us  [the longest x2 0.19 us: shards(): green = green.reshape(near_p, 4, q_size, r_size).transpose(3, 2, 1, 0)]
    all_to_all x15 -> x7, waiting for transfers between devices: 163 us -> 179 us  [exchange(): return lax.all_to_all(sent, 'mom', split_axis=0, concat_axis=0, tiled=True)]
    transpose x1 -> x0, local copies, waits for them, and re-layouts: 11.1 us -> none  [shards(): couple_two = couple_two.reshape(angles, 4, quarter, 4, quarter, 4).transp...]
  transfers between devices with their start and end apart: 15 -> 7, of which waited for: 14 -> 7; matrix products, arithmetic and copies ran while one was open for 6% -> 1% of each run, Pallas kernels for 30% -> 25%
where the time goes in v2:
time: 475 us; the launch traced here: 470 us
  waiting for transfers between devices  179 us (38%)
  Pallas kernels  162 us (34%)
  blocking collectives  75.2 us (16%)
  starting transfers between devices  39.3 us (8%)
  local copies, waits for them, and re-layouts  13.4 us (3%)
    all_to_all x7, waiting for transfers between devices, exchange(): return lax.all_to_all(sent, 'mom', split_axis=0, concat_axis=0, tiled=True)  179 us
    all_to_all x1, blocking collectives, exchange(): return lax.all_to_all(sent, 'mom', split_axis=0, concat_axis=0, tiled=True)  75.2 us
    pallas_call x4, Pallas kernels, component_two(): call(functools.partial(two_kernel, blocks, steps, len(values)), 'componen...  57.5 us
    all_to_all x7, starting transfers between devices, exchange(): return lax.all_to_all(sent, 'mom', split_axis=0, concat_axis=0, tiled=True)  39.3 us
    pallas_call x2, Pallas kernels, first_one(): call(functools.partial(first_kernel, blocks, rows, local), 'component_one...  32.4 us
    pallas_call x2, Pallas kernels, later_one(): call(functools.partial(later_kernel, blocks, steps, len(backs)), 'compone...  32.4 us
    pallas_call x2, Pallas kernels, spline_maps(): call(functools.partial(map_kernel, count), 'spline_maps', 10 * angles * s...  18.1 us
    pallas_call x2, Pallas kernels, amplitude_chunk(): call(functools.partial(amplitude_kernel, quarter), 'amplitude', back.size...  12.9 us
  transfers between devices with their start and end apart: 7, of which 7 were waited for; matrix products, arithmetic and copies ran while one was open for 1% of the time, Pallas kernels for 25%

profile of v2, /device:TPU:9, one launch (start us, length us, event | category | flops | bytes accessed | tf_op | source)
XLA Modules:
  0.0 470.1 jit_solution(4467526428837312193)
XLA Ops:
  0.6 0.7 convert_bitcast_fusion
  1.4 0.8 copy_bitcast_fusion
  2.2 1.4 copy.38.table_ref
  3.6 9.0 %spline_maps.2 = (bf16[1024,2048]{1,0:T(8,128)(2,1)}, bf16[1024,2048]{1,0:T(8,128)(2,1)}) custom-call(f32[2,1024,10]{2,1,0:T(8,128)} %copy.38.table_ref), custom_call_target="tpu_custom_call" | custom-call | flops 20971520 | bytes 8388608 | tf_op jit(solution)/shard_map/spline_maps/pallas_call | solution.py:78
  12.6 12.9 %component_one_first.3 = f32[16,1,2,2,32,128]{5,4,3,2,1,0:T(8,128)} custom-call(f32[8,128,1024]{2,1,0:T(8,128)} %source_ref.7, f32[2,4,128,128]{3,2,1,0:T(8,128)} %refs_2_.6, bf16[1024,2048]{1,0:T(8,128)(2,1)} %get-tuple-element.6.high_ref.refs_3_, bf16[1024,2048]{1,0:T(8,128)(2,1)} %get-tuple-element.7.low_ref.refs_4_), custom_call_target="tpu_custom_call" | custom-call | flops 3623878656 | bytes 12582912 | tf_op jit(solution)/shard_map/component_one_first/pallas_call | solution.py:148
  25.5 6.6 %all-to-all-start.1 = ((f32[16,1,2,64,128]{4,3,2,1,0:T(8,128)}), f32[16,1,2,64,128]{4,3,2,1,0:T(8,128)S(1)}, u32[]{:S(2)}, u32[]{:S(2)}) async-start(f32[16,1,2,64,128]{4,3,2,1,0:T(8,128)} %bitcast.37), calls=%async_computation.1 | async-start | bytes 2097152 | tf_op jit(solution)/shard_map/all_to_all | solution.py:418
  32.1 19.6 %component_one_first.2 = f32[16,3,2,2,32,128]{5,4,3,2,1,0:T(8,128)} custom-call(f32[8,128,1024]{2,1,0:T(8,128)} %source_ref.7, f32[2,4,128,128]{3,2,1,0:T(8,128)} %refs_2_.6, bf16[1024,2048]{1,0:T(8,128)(2,1)} %get-tuple-element.6.high_ref.refs_3_, bf16[1024,2048]{1,0:T(8,128)(2,1)} %get-tuple-element.7.low_ref.refs_4_), custom_call_target="tpu_custom_call" | custom-call | flops 10871635968 | bytes 12582912 | tf_op jit(solution)/shard_map/component_one_first/pallas_call | solution.py:148
  51.7 5.3 %all-to-all-done.1.refs_0_ = f32[16,1,2,64,128]{4,3,2,1,0:T(8,128)S(1)} async-done(((f32[16,1,2,64,128]{4,3,2,1,0:T(8,128)}), f32[16,1,2,64,128]{4,3,2,1,0:T(8,128)S(1)}, u32[]{:S(2)}, u32[]{:S(2)}) %all-to-all-start.1) | async-done | bytes 1048608 | tf_op jit(solution)/shard_map/all_to_all | solution.py:418
  57.0 1.0 copy-done.4
  57.9 4.8 %all-to-all-start = ((f32[16,3,2,64,128]{4,3,2,1,0:T(8,128)}), f32[16,3,2,64,128]{4,3,2,1,0:T(8,128)S(1)}, u32[]{:S(2)}, u32[]{:S(2)}) async-start(f32[16,3,2,64,128]{4,3,2,1,0:T(8,128)} %bitcast.38), calls=%async_computation | async-start | bytes 6291456 | tf_op jit(solution)/shard_map/all_to_all | solution.py:418
  63.4 0.1 copy.39
  63.5 0.1 reshape.81
  63.6 0.1 reshape.84
  63.7 0.1 copy.44
  63.8 0.1 reshape.85
  63.9 0.1 reshape.82
  64.0 0.1 copy.43
  64.1 0.1 reshape.83
  64.3 1.0 copy.47.refs_2_.refs_3_
  65.3 1.4 copy.45.table_ref
  66.7 9.1 %spline_maps.3 = (bf16[1024,2048]{1,0:T(8,128)(2,1)}, bf16[1024,2048]{1,0:T(8,128)(2,1)}) custom-call(f32[2,1024,10]{2,1,0:T(8,128)} %copy.45.table_ref), custom_call_target="tpu_custom_call" | custom-call | flops 20971520 | bytes 8388608 | tf_op jit(solution)/shard_map/spline_maps/pallas_call | solution.py:78
  75.9 10.3 %component_two.4 = f32[16,1,2,2,32,128]{5,4,3,2,1,0:T(8,128)} custom-call(f32[16,1,2,64,128]{4,3,2,1,0:T(8,128)} %copy-done.4, f32[2,4,128,128]{3,2,1,0:T(8,128)} %refs_2_.7, f32[1024,2]{1,0:T(8,128)} %copy.47.refs_2_.refs_3_, bf16[1024,2048]{1,0:T(8,128)(2,1)} %get-tuple-element.8.refs_3_.refs_4_, bf16[1024,2048]{1,0:T(8,128)(2,1)} %get-tuple-element.9.refs_4_.refs_5_), custom_call_target="tpu_custom_call" | custom-call | flops 3623878656 | bytes 9437184 | tf_op jit(solution)/shard_map/component_two/pallas_call | solution.py:308
  86.2 44.3 %all-to-all-done.refs_0_ = f32[16,3,2,64,128]{4,3,2,1,0:T(8,128)S(1)} async-done(((f32[16,3,2,64,128]{4,3,2,1,0:T(8,128)}), f32[16,3,2,64,128]{4,3,2,1,0:T(8,128)S(1)}, u32[]{:S(2)}, u32[]{:S(2)}) %all-to-all-start) | async-done | bytes 3145760 | tf_op jit(solution)/shard_map/all_to_all | solution.py:418
  130.5 6.9 %all-to-all-start.2 = ((f32[16,1,2,64,128]{4,3,2,1,0:T(8,128)}), f32[16,1,2,64,128]{4,3,2,1,0:T(8,128)}, u32[]{:S(2)}, u32[]{:S(2)}) async-start(f32[16,1,2,64,128]{4,3,2,1,0:T(8,128)} %bitcast.41), calls=%async_computation.2 | async-start | bytes 2097152 | tf_op jit(solution)/shard_map/all_to_all | solution.py:418
  137.4 1.0 copy.48.refs_2_.refs_3_
  138.4 17.8 %component_two.5 = f32[16,3,2,2,32,128]{5,4,3,2,1,0:T(8,128)} custom-call(f32[16,3,2,64,128]{4,3,2,1,0:T(8,128)} %copy-done.2, f32[2,4,128,128]{3,2,1,0:T(8,128)} %refs_2_.7, f32[1024,6]{1,0:T(8,128)} %copy.48.refs_2_.refs_3_, bf16[1024,2048]{1,0:T(8,128)(2,1)} %get-tuple-element.8.refs_3_.refs_4_, bf16[1024,2048]{1,0:T(8,128)(2,1)} %get-tuple-element.9.refs_4_.refs_5_), custom_call_target="tpu_custom_call" | custom-call | flops 10871635968 | bytes 11534336 | tf_op jit(solution)/shard_map/component_two/pallas_call | solution.py:308
  156.2 6.2 %all-to-all-done.2.refs_0_ = f32[16,1,2,64,128]{4,3,2,1,0:T(8,128)} async-done(((f32[16,1,2,64,128]{4,3,2,1,0:T(8,128)}), f32[16,1,2,64,128]{4,3,2,1,0:T(8,128)}, u32[]{:S(2)}, u32[]{:S(2)}) %all-to-all-start.2) | async-done | bytes 1048608 | tf_op jit(solution)/shard_map/all_to_all | solution.py:418
  162.4 75.2 %all_to_all.40.refs_1_ = f32[16,3,2,64,128]{4,3,2,1,0:T(8,128)} all-to-all(f32[16,3,2,64,128]{4,3,2,1,0:T(8,128)} %bitcast.40), channel_id=1, replica_groups=mesh['energy'=2,'mom'=16] {'mom'}, dimensions={0} | all-to-all | bytes 6291456 | tf_op jit(solution)/shard_map/all_to_all | solution.py:418
  237.6 11.8 %component_one_later.3 = f32[16,1,2,2,32,128]{5,4,3,2,1,0:T(8,128)} custom-call(f32[16,1,2,64,128]{4,3,2,1,0:T(8,128)} %all-to-all-done.2.refs_0_, f32[16,3,2,64,128]{4,3,2,1,0:T(8,128)} %all_to_all.40.refs_1_, f32[2,4,128,128]{3,2,1,0:T(8,128)} %refs_2_.6, bf16[1024,2048]{1,0:T(8,128)(2,1)} %get-tuple-element.6.high_ref.refs_3_, ...), custom_call_target="tpu_custom_call" | custom-call | flops 4831838208 | bytes 12582912 | tf_op jit(solution)/shard_map/component_one_later/pallas_call | solution.py:230
  249.4 4.6 all-to-all-start.6
  253.9 20.6 %component_one_later.2 = f32[16,3,2,2,32,128]{5,4,3,2,1,0:T(8,128)} custom-call(f32[16,1,2,64,128]{4,3,2,1,0:T(8,128)} %all-to-all-done.2.refs_0_, f32[16,3,2,64,128]{4,3,2,1,0:T(8,128)} %all_to_all.40.refs_1_, f32[2,4,128,128]{3,2,1,0:T(8,128)} %refs_2_.6, bf16[1024,2048]{1,0:T(8,128)(2,1)} %get-tuple-element.6.high_ref.refs_3_, ...), custom_call_target="tpu_custom_call" | custom-call | flops 14495514624 | bytes 12582912 | tf_op jit(solution)/shard_map/component_one_later/pallas_call | solution.py:230
  274.5 4.3 all-to-all-done.6.refs_1_
  278.8 1.0 copy-done.5
  279.8 4.8 %all-to-all-start.4 = ((f32[16,3,2,64,128]{4,3,2,1,0:T(8,128)}), f32[16,3,2,64,128]{4,3,2,1,0:T(8,128)S(1)}, u32[]{:S(2)}, u32[]{:S(2)}) async-start(f32[16,3,2,64,128]{4,3,2,1,0:T(8,128)} %bitcast.39), calls=%async_computation.4 | async-start | bytes 6291456 | tf_op jit(solution)/shard_map/all_to_all | solution.py:418
  284.6 10.6 %component_two.7.sent_ref = f32[16,1,2,2,32,128]{5,4,3,2,1,0:T(8,128)} custom-call(f32[16,1,2,64,128]{4,3,2,1,0:T(8,128)} %copy-done.4, f32[16,1,2,64,128]{4,3,2,1,0:T(8,128)} %copy-done.5, f32[2,4,128,128]{3,2,1,0:T(8,128)} %refs_2_.7, f32[1024,2]{1,0:T(8,128)} %copy.47.refs_2_.refs_3_, bf16[1024,2048]{1,0:T(8,128)(2,1)} %get-tuple-element.8.refs_3_.refs_4_, ...), custom_call_target="tpu_custom_call" | custom-call | flops 3623878656 | bytes 10485760 | tf_op jit(solution)/shard_map/component_two/pallas_call | solution.py:308
  295.2 57.2 %all-to-all-done.4.refs_1_ = f32[16,3,2,64,128]{4,3,2,1,0:T(8,128)S(1)} async-done(((f32[16,3,2,64,128]{4,3,2,1,0:T(8,128)}), f32[16,3,2,64,128]{4,3,2,1,0:T(8,128)S(1)}, u32[]{:S(2)}, u32[]{:S(2)}) %all-to-all-start.4) | async-done | bytes 3145760 | tf_op jit(solution)/shard_map/all_to_all | solution.py:418
  352.3 1.7 copy-done.3
  354.0 6.9 %all-to-all-start.7 = ((f32[16,1,2,64,128]{4,3,2,1,0:T(8,128)}), f32[16,1,2,64,128]{4,3,2,1,0:T(8,128)S(1)}, u32[]{:S(2)}, u32[]{:S(2)}) async-start(f32[16,1,2,64,128]{4,3,2,1,0:T(8,128)} %bitcast.36), calls=%async_computation.7 | async-start | bytes 2097152 | tf_op jit(solution)/shard_map/all_to_all | solution.py:418
  360.9 18.8 %component_two.6.sent_ref = f32[16,3,2,2,32,128]{5,4,3,2,1,0:T(8,128)} custom-call(f32[16,3,2,64,128]{4,3,2,1,0:T(8,128)} %copy-done.2, f32[16,3,2,64,128]{4,3,2,1,0:T(8,128)} %copy-done.3, f32[2,4,128,128]{3,2,1,0:T(8,128)} %refs_2_.7, f32[1024,6]{1,0:T(8,128)} %copy.48.refs_2_.refs_3_, bf16[1024,2048]{1,0:T(8,128)(2,1)} %get-tuple-element.8.refs_3_.refs_4_, ...), custom_call_target="tpu_custom_call" | custom-call | flops 10871635968 | bytes 14680064 | tf_op jit(solution)/shard_map/component_two/pallas_call | solution.py:308
  379.7 6.1 %all-to-all-done.7.back_ref = f32[16,1,2,64,128]{4,3,2,1,0:T(8,128)S(1)} async-done(((f32[16,1,2,64,128]{4,3,2,1,0:T(8,128)}), f32[16,1,2,64,128]{4,3,2,1,0:T(8,128)S(1)}, u32[]{:S(2)}, u32[]{:S(2)}) %all-to-all-start.7) | async-done | bytes 1048608 | tf_op jit(solution)/shard_map/all_to_all | solution.py:418
  385.8 1.0 copy-done.1
  386.8 4.8 %all-to-all-start.5 = ((f32[16,3,2,64,128]{4,3,2,1,0:T(8,128)}), f32[16,3,2,64,128]{4,3,2,1,0:T(8,128)S(1)}, u32[]{:S(2)}, u32[]{:S(2)}) async-start(f32[16,3,2,64,128]{4,3,2,1,0:T(8,128)} %bitcast.35), calls=%async_computation.5 | async-start | bytes 6291456 | tf_op jit(solution)/shard_map/all_to_all | solution.py:418
  391.6 2.6 component_out.2.refs_0_
  394.2 3.8 amplitude.2.refs_0_
  398.0 6.2 %component_out.3 = f32[8,128,1024]{2,1,0:T(8,128)} custom-call(f32[16,3,2,2,32,128]{5,4,3,2,1,0:T(8,128)} %component_two.6.sent_ref, f32[8,128,1024]{2,1,0:T(8,128)} %component_out.2.refs_0_), custom_call_target="tpu_custom_call", output_to_operand_aliasing={{}: (1, {})} | custom-call | bytes 6291456 | tf_op jit(solution)/shard_map/component_out/pallas_call | solution.py:399
  404.2 55.2 %all-to-all-done.5.back_ref = f32[16,3,2,64,128]{4,3,2,1,0:T(8,128)S(1)} async-done(((f32[16,3,2,64,128]{4,3,2,1,0:T(8,128)}), f32[16,3,2,64,128]{4,3,2,1,0:T(8,128)S(1)}, u32[]{:S(2)}, u32[]{:S(2)}) %all-to-all-start.5) | async-done | bytes 3145760 | tf_op jit(solution)/shard_map/all_to_all | solution.py:418
  459.3 1.6 copy-done
  461.0 9.1 %amplitude.3 = f32[8,128,1024]{2,1,0:T(8,128)} custom-call(f32[8,128,1024]{2,1,0:T(8,128)} %source_ref.7, f32[16,3,2,64,128]{4,3,2,1,0:T(8,128)} %copy-done, f32[8,128,1024]{2,1,0:T(8,128)} %amplitude.2.refs_0_), custom_call_target="tpu_custom_call", output_to_operand_aliasing={{}: (2, {})} | custom-call | flops 786432 | bytes 9437184 | tf_op jit(solution)/shard_map/amplitude/pallas_call | solution.py:355
  (30 shorter events, 0.7 us)
Async XLA Ops:
  25.5 31.5 %all-to-all-start.1 = ((f32[16,1,2,64,128]{4,3,2,1,0:T(8,128)}), f32[16,1,2,64,128]{4,3,2,1,0:T(8,128)S(1)}, u32[]{:S(2)}, u32[]{:S(2)}) async-start(f32[16,1,2,64,128]{4,3,2,1,0:T(8,128)} %bitcast.37), calls=%async_computation.1 | async-start | bytes 2097152 | tf_op jit(solution)/shard_map/all_to_all | solution.py:418
  51.6 11.1 %copy-start.9 = (s32[2,1024]{1,0:T(2,128)S(1)}, s32[2,1024]{1,0:T(2,128)}, u32[]{:S(2)}) copy-start(s32[2,1024]{1,0:T(2,128)} %param.20) | copy-start | bytes 24580
  51.6 11.1 %copy-start.10 = (s32[2,1024]{1,0:T(2,128)S(1)}, s32[2,1024]{1,0:T(2,128)}, u32[]{:S(2)}) copy-start(s32[2,1024]{1,0:T(2,128)} %param.21) | copy-start | bytes 24580
  51.6 11.6 %copy-start.6 = (f32[8,1024]{1,0:T(8,128)S(1)}, f32[8,1024]{1,0:T(8,128)}, u32[]{:S(2)}) copy-start(f32[8,1024]{1,0:T(8,128)} %param.13) | copy-start | bytes 98308
  51.6 11.9 %copy-start.7 = (f32[2,4,1024]{2,1,0:T(4,128)S(1)}, f32[2,4,1024]{2,1,0:T(4,128)}, u32[]{:S(2)}) copy-start(f32[2,4,1024]{2,1,0:T(4,128)} %param.22) | copy-start | bytes 98308
  51.7 12.3 %copy-start.8 = (f32[2,4,1024]{2,1,0:T(4,128)S(1)}, f32[2,4,1024]{2,1,0:T(4,128)}, u32[]{:S(2)}) copy-start(f32[2,4,1024]{2,1,0:T(4,128)} %param.23) | copy-start | bytes 98308
  57.0 1.0 copy-start.4
  57.9 72.5 %all-to-all-start = ((f32[16,3,2,64,128]{4,3,2,1,0:T(8,128)}), f32[16,3,2,64,128]{4,3,2,1,0:T(8,128)S(1)}, u32[]{:S(2)}, u32[]{:S(2)}) async-start(f32[16,3,2,64,128]{4,3,2,1,0:T(8,128)} %bitcast.38), calls=%async_computation | async-start | bytes 6291456 | tf_op jit(solution)/shard_map/all_to_all | solution.py:418
  130.5 8.0 %copy-start.2 = (f32[16,3,2,64,128]{4,3,2,1,0:T(8,128)}, f32[16,3,2,64,128]{4,3,2,1,0:T(8,128)S(1)}, u32[]{:S(2)}) copy-start(f32[16,3,2,64,128]{4,3,2,1,0:T(8,128)S(1)} %all-to-all-done.refs_0_) | copy-start | bytes 9437188
  130.5 32.0 %all-to-all-start.2 = ((f32[16,1,2,64,128]{4,3,2,1,0:T(8,128)}), f32[16,1,2,64,128]{4,3,2,1,0:T(8,128)}, u32[]{:S(2)}, u32[]{:S(2)}) async-start(f32[16,1,2,64,128]{4,3,2,1,0:T(8,128)} %bitcast.41), calls=%async_computation.2 | async-start | bytes 2097152 | tf_op jit(solution)/shard_map/all_to_all | solution.py:418
  249.4 29.5 %all-to-all-start.6 = ((f32[16,1,2,64,128]{4,3,2,1,0:T(8,128)}), f32[16,1,2,64,128]{4,3,2,1,0:T(8,128)S(1)}, u32[]{:S(2)}, u32[]{:S(2)}) async-start(f32[16,1,2,64,128]{4,3,2,1,0:T(8,128)} %bitcast.42), calls=%async_computation.6 | async-start | bytes 2097152 | tf_op jit(solution)/shard_map/all_to_all | solution.py:418
  278.8 1.0 copy-start.5
  279.8 72.5 %all-to-all-start.4 = ((f32[16,3,2,64,128]{4,3,2,1,0:T(8,128)}), f32[16,3,2,64,128]{4,3,2,1,0:T(8,128)S(1)}, u32[]{:S(2)}, u32[]{:S(2)}) async-start(f32[16,3,2,64,128]{4,3,2,1,0:T(8,128)} %bitcast.39), calls=%async_computation.4 | async-start | bytes 6291456 | tf_op jit(solution)/shard_map/all_to_all | solution.py:418
  352.3 1.7 copy-start.3
  354.0 31.8 %all-to-all-start.7 = ((f32[16,1,2,64,128]{4,3,2,1,0:T(8,128)}), f32[16,1,2,64,128]{4,3,2,1,0:T(8,128)S(1)}, u32[]{:S(2)}, u32[]{:S(2)}) async-start(f32[16,1,2,64,128]{4,3,2,1,0:T(8,128)} %bitcast.36), calls=%async_computation.7 | async-start | bytes 2097152 | tf_op jit(solution)/shard_map/all_to_all | solution.py:418
  385.8 1.0 copy-start.1
  386.8 72.5 %all-to-all-start.5 = ((f32[16,3,2,64,128]{4,3,2,1,0:T(8,128)}), f32[16,3,2,64,128]{4,3,2,1,0:T(8,128)S(1)}, u32[]{:S(2)}, u32[]{:S(2)}) async-start(f32[16,3,2,64,128]{4,3,2,1,0:T(8,128)} %bitcast.35), calls=%async_computation.5 | async-start | bytes 6291456 | tf_op jit(solution)/shard_map/all_to_all | solution.py:418
  459.3 1.6 copy-start
